TPU v7x, 32 devices: a whole 2x2x4 slice. The times are simulated.
32 devices in a mesh: dp: 4 (over y, x), seq: 4 (over z), tensor: 2 (over core).
Axes of the slice: x: 2, y: 2, z: 4, core: 2. Of those that a mesh axis runs over, the one named last changes fastest.
Arguments:
- hidden: bfloat16 [8, 1024, 768], P('dp', 'seq'), may hold values from -6 to 6
- cotangent: bfloat16 [8, 1024, 768], P('dp', 'seq'), may hold values from -6 to 6
- gating: float32 [768, 1536], P(('dp', 'seq'), 'tensor'), may hold values from -0.21875 to 0.21875
- values: float32 [768, 1536], P(('dp', 'seq'), 'tensor'), may hold values from -0.21875 to 0.21875
- selector: float32 [768, 256], P(('dp', 'seq'), 'tensor'), may hold values from -0.21875 to 0.21875
- timestep: float32 [768, 24], P(('dp', 'seq'), 'tensor'), may hold values from -0.4375 to 0.4375
- output: float32 [1536, 768], P('tensor', ('dp', 'seq')), may hold values from -0.15625 to 0.15625
- prenorm: float32 [768], P(('dp', 'seq')), may hold values from 0.5 to 1.5
- postnorm: float32 [1536], P('tensor'), may hold values from 0.5 to 1.5
- filters: float32 [5, 1536], P(None, 'tensor'), may hold values from -3 to 3
- kernels: float32 [5, 256], P(None, 'tensor'), may hold values from -3 to 3
- scalars: float32 [3, 24], P(None, 'tensor'), may hold values from -14 to 2
- gating_adam: float32 [2, 768, 1536], P(None, ('dp', 'seq'), 'tensor'), may hold values from -2 to 2, as said below
- values_adam: float32 [2, 768, 1536], P(None, ('dp', 'seq'), 'tensor'), may hold values from -2 to 2, as said below
- selector_adam: float32 [2, 768, 256], P(None, ('dp', 'seq'), 'tensor'), may hold values from -2 to 2, as said below
- timestep_adam: float32 [2, 768, 24], P(None, ('dp', 'seq'), 'tensor'), may hold values from -2 to 2, as said below
- output_adam: float32 [2, 1536, 768], P(None, 'tensor', ('dp', 'seq')), may hold values from -2 to 2, as said below
- prenorm_adam: float32 [2, 768], P(None, ('dp', 'seq')), may hold values from -97 to 97, as said below
- postnorm_adam: float32 [2, 1536], P(None, 'tensor'), may hold values from -2 to 2, as said below
- filters_adam: float32 [2, 5, 1536], P(None, None, 'tensor'), may hold values from -2 to 2, as said below
- kernels_adam: float32 [2, 5, 256], P(None, None, 'tensor'), may hold values from -2 to 2, as said below
- scalars_adam: float32 [2, 3, 24], P(None, None, 'tensor'), may hold values from -2 to 2, as said below
Outputs:
- result: float32 [8, 1024, 768], P('dp', 'seq')
- hidden_grad: float32 [8, 1024, 768], P('dp', 'seq')
- gating_grad: float32 [768, 1536], P(('dp', 'seq'), 'tensor')
- values_grad: float32 [768, 1536], P(('dp', 'seq'), 'tensor')
- selector_grad: float32 [768, 256], P(('dp', 'seq'), 'tensor')
- timestep_grad: float32 [768, 24], P(('dp', 'seq'), 'tensor')
- output_grad: float32 [1536, 768], P('tensor', ('dp', 'seq'))
- prenorm_grad: float32 [768], P(('dp', 'seq'))
- postnorm_grad: float32 [1536], P('tensor')
- filters_grad: float32 [5, 1536], P(None, 'tensor')
- kernels_grad: float32 [5, 256], P(None, 'tensor')
- scalars_grad: float32 [3, 24], P(None, 'tensor')
- gating_next: float32 [768, 1536], P(('dp', 'seq'), 'tensor')
- values_next: float32 [768, 1536], P(('dp', 'seq'), 'tensor')
- selector_next: float32 [768, 256], P(('dp', 'seq'), 'tensor')
- timestep_next: float32 [768, 24], P(('dp', 'seq'), 'tensor')
- output_next: float32 [1536, 768], P('tensor', ('dp', 'seq'))
- prenorm_next: float32 [768], P(('dp', 'seq'))
- postnorm_next: float32 [1536], P('tensor')
- filters_next: float32 [5, 1536], P(None, 'tensor')
- kernels_next: float32 [5, 256], P(None, 'tensor')
- scalars_next: float32 [3, 24], P(None, 'tensor')
- gating_state: float32 [2, 768, 1536], P(None, ('dp', 'seq'), 'tensor')
- values_state: float32 [2, 768, 1536], P(None, ('dp', 'seq'), 'tensor')
- selector_state: float32 [2, 768, 256], P(None, ('dp', 'seq'), 'tensor')
- timestep_state: float32 [2, 768, 24], P(None, ('dp', 'seq'), 'tensor')
- output_state: float32 [2, 1536, 768], P(None, 'tensor', ('dp', 'seq'))
- prenorm_state: float32 [2, 768], P(None, ('dp', 'seq'))
- postnorm_state: float32 [2, 1536], P(None, 'tensor')
- filters_state: float32 [2, 5, 1536], P(None, None, 'tensor')
- kernels_state: float32 [2, 5, 256], P(None, None, 'tensor')
- scalars_state: float32 [2, 3, 24], P(None, None, 'tensor')
Inputs may be any that keep to these rules, and one draw needn't show every extreme that they name: `gating_adam`: index 1 is positive. `values_adam`: index 1 is positive. `selector_adam`: index 1 is positive. `timestep_adam`: index 1 is positive. `output_adam`: index 1 is positive. `prenorm_adam`: index 1 is positive. `postnorm_adam`: index 1 is positive. `filters_adam`: index 1 is positive. `kernels_adam`: index 1 is positive. `scalars_adam`: index 1 is positive.
All inputs are finite; a program needn't handle non-finite values.
Results may differ from a plain program's by a relative error of at most 0.015.
The roundings to bfloat16 on the way count: a program that leaves them out, or rounds other values in their place, can miss the bound.
Values may be sent and summed in bfloat16 or wider, within the bound.
A program may use at most 128 MiB of HBM per device.

v0:
```python
import jax
import jax.numpy as jnp
from jax import lax
from jax.sharding import PartitionSpec as P

INNER = 1536
STATE = 128
HEADDIM = 64
STEP = 2


epsilon = 1e-05
highest = lax.Precision.HIGHEST
learn_rate = 0.01
first_decay = 0.9
second_decay = 0.999
adam_epsilon = 1e-08
weight_decay = 0.1


def from_behind(block, axis, distance):
    devices = range(lax.axis_size(axis))
    route = [(i - distance, i) for i in devices if i - distance in devices]
    return lax.ppermute(block, axis, route)


def carried_in(value, axis, join, neutral, backward):
    count, mine = (lax.axis_size(axis), lax.axis_index(axis))
    pieces = jax.tree.map(lambda part: lax.all_gather(part, axis), value)
    if backward:
        pieces = jax.tree.map(lambda part: part[::-1], pieces)
        mine = count - 1 - mine
    so_far = jax.tree.map(
        lambda part, zero: jnp.full_like(part, 0) + jnp.asarray(zero, part.dtype), value, neutral
    )

    def hop(position, so_far):
        longer = join(so_far, jax.tree.map(lambda part: part[position], pieces))
        return jax.tree.map(lambda new, old: jnp.where(position < mine, new, old), longer, so_far)

    return lax.fori_loop(0, count - 1, hop, so_far)


def swish_parts(value):
    sigmoid = jax.nn.sigmoid(value)
    return (value * sigmoid, sigmoid * (1.0 + value * (1.0 - sigmoid)))


def conv_apply(padded, taps):
    tap_count = taps.shape[0] - 1
    length = padded.shape[1] - tap_count + 1
    wide = padded.astype(jnp.float32)
    total = taps[tap_count] + taps[0] * wide[:, 0:length]
    for index in range(1, tap_count):
        total = total + taps[index] * wide[:, index : index + length]
    return total


def conv_back(padded, taps, grad_pre):
    tap_count = taps.shape[0] - 1
    length = grad_pre.shape[1]
    wide = padded.astype(jnp.float32)
    tap_rows = [
        jnp.sum(grad_pre * wide[:, index : index + length], axis=(0, 1))
        for index in range(tap_count)
    ]
    tap_rows.append(jnp.sum(grad_pre, axis=(0, 1)))
    grad_pad = jnp.zeros(padded.shape, jnp.float32)
    for index in range(tap_count):
        grad_pad = grad_pad + jnp.pad(
            taps[index] * grad_pre, ((0, 0), (index, tap_count - 1 - index), (0, 0))
        )
    return (jnp.stack(tap_rows), grad_pad)


def group_terms(inner, write_vec, read_vec, delta, running):
    length = inner.shape[1]
    scores = jnp.einsum("btn,bun->btu", read_vec, write_vec, preferred_element_type=jnp.float32)
    causal = jnp.arange(length)[:, None] >= jnp.arange(length)[None, :]
    by_head = jnp.transpose(running, (0, 2, 1))
    gap = by_head[:, :, :, None] - by_head[:, :, None, :]
    decays = jnp.exp(jnp.where(causal, gap, -jnp.inf))
    step_head = jnp.transpose(delta, (0, 2, 1))
    mixing = scores[:, None] * decays * step_head[:, :, None, :]
    mixing_b = mixing.astype(jnp.bfloat16)
    within = jnp.einsum("bhtu,buhp->bthp", mixing_b, inner, preferred_element_type=jnp.float32)
    inner_f = inner.astype(jnp.float32)
    weight_end = jnp.exp(running[:, -1:, :] - running) * delta
    local_state = jnp.einsum(
        "bthp,btn->bhpn",
        inner_f * weight_end[..., None],
        write_vec.astype(jnp.float32),
        precision=highest,
    )
    carry_decay = jnp.exp(running[:, -1, :])
    return (scores, decays, mixing_b, within, weight_end, local_state, carry_decay)


def group_back_first(
    inner, write_vec, read_vec, delta, running, skip, entering, grad_mixer, scores, decays, mixing_b
):
    grad_half = grad_mixer.astype(jnp.bfloat16)
    inner_f = inner.astype(jnp.float32)
    write_f = write_vec.astype(jnp.float32)
    read_f = read_vec.astype(jnp.float32)
    skip_grad = jnp.sum(grad_mixer * inner_f, axis=(0, 1, 3))
    grad_inner = skip[None, None, :, None] * grad_mixer + jnp.einsum(
        "bhtu,bthp->buhp", mixing_b, grad_half, preferred_element_type=jnp.float32
    )
    grad_mix = jnp.einsum("bthp,buhp->bhtu", grad_half, inner, preferred_element_type=jnp.float32)
    step_head = jnp.transpose(delta, (0, 2, 1))
    kernel = grad_mix * decays * scores[:, None]
    grad_delta = jnp.transpose(jnp.sum(kernel, axis=2), (0, 2, 1))
    weighted = kernel * step_head[:, :, None, :]
    grad_running = jnp.transpose(jnp.sum(weighted, axis=3) - jnp.sum(weighted, axis=2), (0, 2, 1))
    grad_scores = jnp.sum(grad_mix * decays * step_head[:, :, None, :], axis=1)
    grad_read = jnp.einsum("btu,bun->btn", grad_scores, write_f, precision=highest)
    grad_write = jnp.einsum("btu,btn->bun", grad_scores, read_f, precision=highest)
    growth = jnp.exp(running)
    across = jnp.einsum("btn,bhpn->bthp", read_f, entering, precision=highest)
    grad_running = grad_running + jnp.sum(grad_mixer * across, axis=3) * growth
    scaled = grad_mixer * growth[..., None]
    grad_read = grad_read + jnp.einsum("bthp,bhpn->btn", scaled, entering, precision=highest)
    pushed = jnp.einsum("bthp,btn->bhpn", scaled, read_f, precision=highest)
    return (grad_inner, grad_delta, grad_running, grad_write, grad_read, skip_grad, pushed)


def group_back_second(
    inner,
    write_vec,
    running,
    weight_end,
    entering,
    carry_decay,
    end_grad,
    grad_inner,
    grad_delta,
    grad_running,
    grad_write,
):
    inner_f = inner.astype(jnp.float32)
    write_f = write_vec.astype(jnp.float32)
    decay_grad = jnp.sum(end_grad * entering, axis=(2, 3))
    end_extra = decay_grad * carry_decay
    grad_xw = jnp.einsum("bhpn,btn->bthp", end_grad, write_f, precision=highest)
    grad_write = grad_write + jnp.einsum(
        "bhpn,bthp->btn", end_grad, inner_f * weight_end[..., None], precision=highest
    )
    grad_inner = grad_inner + grad_xw * weight_end[..., None]
    grad_weight = jnp.sum(grad_xw * inner_f, axis=3)
    grad_delta = grad_delta + grad_weight * jnp.exp(running[:, -1:, :] - running)
    spread = grad_weight * weight_end
    end_extra = end_extra + jnp.sum(spread, axis=1)
    grad_running = grad_running - spread
    grad_running = jnp.concatenate(
        [grad_running[:, :-1], grad_running[:, -1:] + end_extra[:, None]], axis=1
    )
    grad_log = jnp.flip(jnp.cumsum(jnp.flip(grad_running, 1), axis=1), 1)
    return (grad_inner, grad_delta, grad_write, grad_log)


def combine(earlier, later):
    return (earlier[0] * later[0], later[0][:, :, None, None] * earlier[1] + later[1])


def adamw(param, moments, grad):
    first = first_decay * moments[0] + (1.0 - first_decay) * grad
    second = second_decay * moments[1] + (1.0 - second_decay) * grad * grad
    first_hat = first / (1.0 - first_decay**STEP)
    second_hat = second / (1.0 - second_decay**STEP)
    fresh = param - learn_rate * (
        first_hat / (jnp.sqrt(second_hat) + adam_epsilon) + weight_decay * param
    )
    return (fresh, jnp.stack([first, second]))


def shards(
    hidden,
    cotangent,
    gating,
    values,
    selector,
    timestep,
    output,
    prenorm,
    postnorm,
    filters,
    kernels,
    scalars,
    gating_adam,
    values_adam,
    selector_adam,
    timestep_adam,
    output_adam,
    prenorm_adam,
    postnorm_adam,
    filters_adam,
    kernels_adam,
    scalars_adam,
):
    half = jnp.bfloat16
    single = jnp.float32
    gate_half = gating.astype(half)
    value_half = values.astype(half)
    select_half = selector.astype(half)
    delta_whalf = timestep.astype(half)
    out_half = output.astype(half)
    gain_half = prenorm.astype(half)
    gathered = (
        lax.all_gather(gate_half, ("dp", "seq"), axis=0, tiled=True),
        lax.all_gather(value_half, ("dp", "seq"), axis=0, tiled=True),
        lax.all_gather(select_half, ("dp", "seq"), axis=0, tiled=True),
        lax.all_gather(delta_whalf, ("dp", "seq"), axis=0, tiled=True),
        lax.all_gather(out_half, ("dp", "seq"), axis=1, tiled=True),
        lax.all_gather(gain_half, ("dp", "seq"), axis=0, tiled=True),
    )
    gate_weight, value_weight, select_weight, delta_weight, out_weight, entry_half = gathered
    seqs_dev, length, width = hidden.shape
    rows = seqs_dev * length
    lead = filters.shape[0] - 2
    heads_here = timestep.shape[1]
    inner_here = gating.shape[1]
    select_here = selector.shape[1]
    bias = scalars[0]
    rate = -jnp.exp(scalars[1])
    skip = scalars[2]
    entry_gain = entry_half.astype(single)
    residual = hidden.astype(single)
    entry_scale = lax.rsqrt(jnp.mean(residual * residual, axis=-1, keepdims=True) + epsilon)
    normed = (residual * entry_scale * entry_gain).astype(half)
    flat = normed.reshape(rows, width)
    gate_raw = (
        jnp.dot(flat, gate_weight, preferred_element_type=single)
        .astype(half)
        .reshape(seqs_dev, length, inner_here)
    )
    inner_raw = (
        jnp.dot(flat, value_weight, preferred_element_type=single)
        .astype(half)
        .reshape(seqs_dev, length, inner_here)
    )
    select_raw = (
        jnp.dot(flat, select_weight, preferred_element_type=single)
        .astype(half)
        .reshape(seqs_dev, length, select_here)
    )
    delta_raw = jnp.dot(flat, delta_weight, preferred_element_type=single).reshape(
        seqs_dev, length, heads_here
    )
    tails = from_behind((inner_raw[:, length - lead :], select_raw[:, length - lead :]), "seq", 1)
    inner_pad = jnp.concatenate([tails[0], inner_raw], axis=1)
    select_pad = jnp.concatenate([tails[1], select_raw], axis=1)
    inner_value, inner_slope = swish_parts(conv_apply(inner_pad, filters))
    select_value, select_slope = swish_parts(conv_apply(select_pad, kernels))
    inner_act = inner_value.astype(half)
    both = lax.all_gather(select_value.astype(half), "tensor", axis=2, tiled=True)
    write_vec = both[:, :, :STATE]
    read_vec = both[:, :, STATE:]
    delta = jax.nn.softplus(delta_raw + bias)
    running = jnp.cumsum(delta * rate, axis=1)
    inner_h = inner_act.reshape(seqs_dev, length, heads_here, HEADDIM)
    scores, decays, mixing_b, within, weight_end, local_state, carry_decay = group_terms(
        inner_h, write_vec, read_vec, delta, running
    )
    entering = carried_in(
        (carry_decay, local_state),
        "seq",
        combine,
        (jnp.ones_like(carry_decay), jnp.zeros_like(local_state)),
        False,
    )[1]
    inner_f = inner_h.astype(single)
    read_f = read_vec.astype(single)
    growth = jnp.exp(running)
    across = jnp.einsum("btn,bhpn->bthp", read_f, entering, precision=highest)
    mixer_out = (within + growth[..., None] * across + skip[None, None, :, None] * inner_f).reshape(
        seqs_dev, length, inner_here
    )
    gate_act, gate_slope = swish_parts(gate_raw.astype(single))
    gated = mixer_out * gate_act
    squares = lax.psum(jnp.sum(gated * gated, axis=-1), "tensor")
    gate_scale = lax.rsqrt(squares / INNER + epsilon)[..., None]
    mixed = (gated * gate_scale * postnorm).astype(half)
    mixed_flat = mixed.reshape(rows, inner_here)
    branch = lax.psum(jnp.dot(mixed_flat, out_weight, preferred_element_type=single), "tensor")
    result = residual + branch.reshape(seqs_dev, length, width)
    late = lax.optimization_barrier(
        ((gate_half, value_half, select_half, delta_whalf, out_half, gain_half), result)
    )[0]
    regathered = (
        lax.all_gather(late[0], ("dp", "seq"), axis=0, tiled=True),
        lax.all_gather(late[1], ("dp", "seq"), axis=0, tiled=True),
        lax.all_gather(late[2], ("dp", "seq"), axis=0, tiled=True),
        lax.all_gather(late[3], ("dp", "seq"), axis=0, tiled=True),
        lax.all_gather(late[4], ("dp", "seq"), axis=1, tiled=True),
        lax.all_gather(late[5], ("dp", "seq"), axis=0, tiled=True),
    )
    gate_weight, value_weight, select_weight, delta_weight, out_weight, entry_half = regathered
    entry_gain = entry_half.astype(single)
    upstream = cotangent.reshape(rows, width)
    grad_mixed = jnp.dot(upstream, out_weight.T, preferred_element_type=single).reshape(
        seqs_dev, length, inner_here
    )
    output_grad = jnp.dot(mixed_flat.T, upstream, preferred_element_type=single)
    postnorm_grad = jnp.sum(grad_mixed * gated * gate_scale, axis=(0, 1))
    hat_gated = grad_mixed * postnorm
    dots = lax.psum(jnp.sum(hat_gated * gated, axis=-1), "tensor")
    cube = gate_scale * gate_scale * gate_scale
    grad_gated = gate_scale * hat_gated - gated * cube * (dots / INNER)[..., None]
    grad_mixer = (grad_gated * gate_act).reshape(seqs_dev, length, heads_here, HEADDIM)
    grad_gate = (grad_gated * mixer_out * gate_slope).astype(half).reshape(rows, inner_here)
    grad_inner, grad_delta, grad_running, grad_write, grad_read, skip_grad, pushed = (
        group_back_first(
            inner_h,
            write_vec,
            read_vec,
            delta,
            running,
            skip,
            entering,
            grad_mixer,
            scores,
            decays,
            mixing_b,
        )
    )
    end_grad = carried_in(
        (carry_decay, pushed),
        "seq",
        combine,
        (jnp.ones_like(carry_decay), jnp.zeros_like(pushed)),
        True,
    )[1]
    grad_inner, grad_delta, grad_write, grad_log = group_back_second(
        inner_h,
        write_vec,
        running,
        weight_end,
        entering,
        carry_decay,
        end_grad,
        grad_inner,
        grad_delta,
        grad_running,
        grad_write,
    )
    grad_delta = grad_delta + grad_log * rate
    alog_grad = jnp.sum(grad_log * delta, axis=(0, 1)) * rate
    grad_delta_pre = grad_delta * jax.nn.sigmoid(delta_raw + bias)
    bias_grad = jnp.sum(grad_delta_pre, axis=(0, 1))
    grad_select = lax.psum_scatter(
        jnp.concatenate([grad_write, grad_read], axis=2), "tensor", scatter_dimension=2, tiled=True
    )
    filters_grad, inner_pad_grad = conv_back(
        inner_pad, filters, grad_inner.reshape(seqs_dev, length, inner_here) * inner_slope
    )
    kernels_grad, select_pad_grad = conv_back(select_pad, kernels, grad_select * select_slope)
    back = from_behind((inner_pad_grad[:, :lead], select_pad_grad[:, :lead]), "seq", -1)
    inner_raw_grad = (
        jnp.concatenate(
            [inner_pad_grad[:, lead:length], inner_pad_grad[:, length:] + back[0]], axis=1
        )
        .astype(half)
        .reshape(rows, inner_here)
    )
    select_raw_grad = (
        jnp.concatenate(
            [select_pad_grad[:, lead:length], select_pad_grad[:, length:] + back[1]], axis=1
        )
        .astype(half)
        .reshape(rows, select_here)
    )
    delta_half = grad_delta_pre.astype(half).reshape(rows, heads_here)
    grad_part = jnp.dot(grad_gate, gate_weight.T, preferred_element_type=single)
    grad_part = grad_part + jnp.dot(inner_raw_grad, value_weight.T, preferred_element_type=single)
    grad_part = grad_part + jnp.dot(select_raw_grad, select_weight.T, preferred_element_type=single)
    grad_part = grad_part + jnp.dot(delta_half, delta_weight.T, preferred_element_type=single)
    grad_normed = lax.psum(grad_part, "tensor").reshape(seqs_dev, length, width)
    gating_grad = jnp.dot(flat.T, grad_gate, preferred_element_type=single)
    values_grad = jnp.dot(flat.T, inner_raw_grad, preferred_element_type=single)
    selector_grad = jnp.dot(flat.T, select_raw_grad, preferred_element_type=single)
    timestep_grad = jnp.dot(flat.T, delta_half, preferred_element_type=single)
    prenorm_grad = jnp.sum(grad_normed * residual * entry_scale, axis=(0, 1))
    hat = grad_normed * entry_gain
    hidden_grad = (
        cotangent.astype(single)
        + entry_scale * hat
        - residual
        * entry_scale
        * entry_scale
        * entry_scale
        * jnp.mean(hat * residual, axis=-1, keepdims=True)
    )
    summed = (
        lax.psum_scatter(gating_grad, ("dp", "seq"), scatter_dimension=0, tiled=True),
        lax.psum_scatter(values_grad, ("dp", "seq"), scatter_dimension=0, tiled=True),
        lax.psum_scatter(selector_grad, ("dp", "seq"), scatter_dimension=0, tiled=True),
        lax.psum_scatter(timestep_grad, ("dp", "seq"), scatter_dimension=0, tiled=True),
        lax.psum_scatter(output_grad, ("dp", "seq"), scatter_dimension=1, tiled=True),
        lax.psum_scatter(prenorm_grad, ("dp", "seq"), scatter_dimension=0, tiled=True),
    )
    scalars_local = jnp.stack([bias_grad, alog_grad, skip_grad])
    small = lax.psum((filters_grad, kernels_grad, scalars_local, postnorm_grad), ("dp", "seq"))
    grads = (
        summed[0],
        summed[1],
        summed[2],
        summed[3],
        summed[4],
        summed[5],
        small[3],
        small[0],
        small[1],
        small[2],
    )
    params = (
        gating,
        values,
        selector,
        timestep,
        output,
        prenorm,
        postnorm,
        filters,
        kernels,
        scalars,
    )
    moments = (
        gating_adam,
        values_adam,
        selector_adam,
        timestep_adam,
        output_adam,
        prenorm_adam,
        postnorm_adam,
        filters_adam,
        kernels_adam,
        scalars_adam,
    )
    updated = [adamw(param, moment, grad) for param, moment, grad in zip(params, moments, grads)]
    return (
        result,
        hidden_grad,
        grads[0],
        grads[1],
        grads[2],
        grads[3],
        grads[4],
        grads[5],
        grads[6],
        grads[7],
        grads[8],
        grads[9],
        updated[0][0],
        updated[1][0],
        updated[2][0],
        updated[3][0],
        updated[4][0],
        updated[5][0],
        updated[6][0],
        updated[7][0],
        updated[8][0],
        updated[9][0],
        updated[0][1],
        updated[1][1],
        updated[2][1],
        updated[3][1],
        updated[4][1],
        updated[5][1],
        updated[6][1],
        updated[7][1],
        updated[8][1],
        updated[9][1],
    )


def solution(mesh):
    placed = (
        P("dp", "seq", None),
        P("dp", "seq", None),
        P(("dp", "seq"), "tensor"),
        P(("dp", "seq"), "tensor"),
        P(("dp", "seq"), "tensor"),
        P(("dp", "seq"), "tensor"),
        P("tensor", ("dp", "seq")),
        P(("dp", "seq")),
        P("tensor"),
        P(None, "tensor"),
        P(None, "tensor"),
        P(None, "tensor"),
        P(None, ("dp", "seq"), "tensor"),
        P(None, ("dp", "seq"), "tensor"),
        P(None, ("dp", "seq"), "tensor"),
        P(None, ("dp", "seq"), "tensor"),
        P(None, "tensor", ("dp", "seq")),
        P(None, ("dp", "seq")),
        P(None, "tensor"),
        P(None, None, "tensor"),
        P(None, None, "tensor"),
        P(None, None, "tensor"),
    )
    return jax.shard_map(
        shards,
        mesh=mesh,
        in_specs=placed,
        out_specs=(
            P("dp", "seq", None),
            P("dp", "seq", None),
            P(("dp", "seq"), "tensor"),
            P(("dp", "seq"), "tensor"),
            P(("dp", "seq"), "tensor"),
            P(("dp", "seq"), "tensor"),
            P("tensor", ("dp", "seq")),
            P(("dp", "seq")),
            P("tensor"),
            P(None, "tensor"),
            P(None, "tensor"),
            P(None, "tensor"),
            P(("dp", "seq"), "tensor"),
            P(("dp", "seq"), "tensor"),
            P(("dp", "seq"), "tensor"),
            P(("dp", "seq"), "tensor"),
            P("tensor", ("dp", "seq")),
            P(("dp", "seq")),
            P("tensor"),
            P(None, "tensor"),
            P(None, "tensor"),
            P(None, "tensor"),
            P(None, ("dp", "seq"), "tensor"),
            P(None, ("dp", "seq"), "tensor"),
            P(None, ("dp", "seq"), "tensor"),
            P(None, ("dp", "seq"), "tensor"),
            P(None, "tensor", ("dp", "seq")),
            P(None, ("dp", "seq")),
            P(None, "tensor"),
            P(None, None, "tensor"),
            P(None, None, "tensor"),
            P(None, None, "tensor"),
        ),
        check_vma=False,
    )
```

profile of v0, /device:TPU:11, one launch (start us, length us, event | category | flops | bytes accessed | tf_op | source)
XLA Modules:
  0.0 1272.0 jit_solution(5869166371537818580)
XLA Ops:
  11.9 27.1 %all-reduce.8 = bf16[768]{0:T(1024)(128)(2,1)S(1)} all-reduce(bf16[768]{0:T(1024)(128)(2,1)S(1)} %dynamic-update-slice), channel_id=1, replica_groups=mesh['dp'=4,'seq'=4,'tensor'=2] {'dp','seq'}, use_global_device_ids=true, to_apply=%add.8 | all-reduce | flops 768 | bytes 3072
  39.7 33.2 %all_gather.59 = bf16[768,128]{1,0:T(8,128)(2,1)S(1)} all-gather(bf16[48,128]{1,0:T(8,128)(2,1)S(1)} %convert_element_type.145), channel_id=1, replica_groups=mesh['dp'=4,'seq'=4,'tensor'=2] {'dp','seq'}, dimensions={0}, use_global_device_ids=true | all-gather | bytes 208896 | tf_op jit(solution)/shard_map/all_gather | solution.py:212
  80.9 27.9 %all-gather.3 = bf16[16,48,12]{1,2,0:T(8,128)(2,1)S(1)} all-gather(bf16[1,48,12]{1,2,0:T(8,128)(2,1)S(1)} %convert_bitcast_fusion), channel_id=1, replica_groups=mesh['dp'=4,'seq'=4,'tensor'=2] {'dp','seq'}, dimensions={0}, use_global_device_ids=true | all-gather | bytes 19584 | tf_op jit(solution)/shard_map/all_gather | solution.py:213
  123.4 24.1 %all_gather.60 = bf16[2,256,256]{2,1,0:T(8,128)(2,1)} all-gather(bf16[2,256,128]{2,1,0:T(8,128)(2,1)S(1)} %get-tuple-element.492), channel_id=1, replica_groups=mesh['dp'=4,'seq'=4,'tensor'=2] {'tensor'}, dimensions={2}, use_global_device_ids=true | all-gather | bytes 393216 | tf_op jit(solution)/shard_map/all_gather | solution.py:256
  157.8 7.6 all-gather
  177.4 39.5 %all-gather.26.cloned.1.call-done = f32[8,12,64,128]{3,2,1,0:T(8,128)} async-done(((f32[2,12,64,128]{3,2,1,0:T(8,128)}), f32[8,12,64,128]{3,2,1,0:T(8,128)}) %all-gather.26.cloned.1.call-update) | async-done | bytes 3145744 | tf_op jit(solution)/shard_map/all_gather | solution.py:29
  237.4 127.8 %reduce-scatter.17.cloned.1.call-done = f32[768,48]{0,1:T(8,128)} async-done(((f32[768,768]{0,1:T(8,128)}), f32[768,48]{0,1:T(8,128)}) %reduce-scatter.17.cloned.1.call-update) | async-done | bytes 147472 | tf_op jit(solution)/shard_map/reduce_scatter | solution.py:399
  374.0 48.5 %all-gather.18.cloned.1.call-done = bf16[768,768]{0,1:T(8,128)(2,1)} async-done(((bf16[768,48]{0,1:T(8,128)(2,1)}), bf16[768,768]{0,1:T(8,128)(2,1)}) %all-gather.18.cloned.1.call-update) | async-done | bytes 1179664 | tf_op jit(solution)/shard_map/all_gather | solution.py:214
  427.7 22.0 %all-reduce.15.cloned.1.call-done = f32[2,256,768]{2,1,0:T(8,128)} async-done(((f32[2,256,768]{2,1,0:T(8,128)}), f32[2,256,768]{2,1,0:T(8,128)}) %all-reduce.15.cloned.1.call-update) | async-done | bytes 1572880 | tf_op jit(solution)/shard_map/psum | solution.py:285
  453.3 53.5 %all-gather.20.cloned.1.call-done = bf16[768,768]{0,1:T(8,128)(2,1)} async-done(((bf16[768,48]{0,1:T(8,128)(2,1)}), bf16[768,768]{0,1:T(8,128)(2,1)}) %all-gather.20.cloned.1.call-update) | async-done | bytes 1179664 | tf_op jit(solution)/shard_map/all_gather | solution.py:295
  506.9 5.2 multiply_reduce_fusion.8
  530.2 5.9 multiply_reduce_fusion.1
  540.0 50.0 %all-gather.28.cloned.1.call-done = f32[8,12,64,128]{3,2,1,0:T(8,128)} async-done(((f32[2,12,64,128]{3,2,1,0:T(8,128)}), f32[8,12,64,128]{3,2,1,0:T(8,128)}) %all-gather.28.cloned.1.call-update) | async-done | bytes 3145744 | tf_op jit(solution)/shard_map/all_gather | solution.py:29
  604.9 32.0 %all_gather.72 = bf16[768,128]{1,0:T(8,128)(2,1)} all-gather(bf16[48,128]{1,0:T(8,128)(2,1)S(1)} %convert_element_type.145), channel_id=1, replica_groups=mesh['dp'=4,'seq'=4,'tensor'=2] {'dp','seq'}, dimensions={0}, use_global_device_ids=true | all-gather | bytes 208896 | tf_op jit(solution)/shard_map/all_gather | solution.py:293
  636.9 5.4 convolution_bitcast_fusion.2
  643.0 29.0 %all-gather.4 = bf16[16,48,12]{1,2,0:T(8,128)(2,1)S(1)} all-gather(bf16[1,48,12]{1,2,0:T(8,128)(2,1)S(1)} %bitcast.421), channel_id=1, replica_groups=mesh['dp'=4,'seq'=4,'tensor'=2] {'dp','seq'}, dimensions={0}, use_global_device_ids=true | all-gather | bytes 19584 | tf_op jit(solution)/shard_map/all_gather | solution.py:294
  677.6 5.6 fusion.43
  740.6 31.1 %all-reduce.9 = bf16[768]{0:T(1024)(128)(2,1)S(1)} all-reduce(bf16[768]{0:T(1024)(128)(2,1)S(1)} %dynamic-update-slice.1), channel_id=1, replica_groups=mesh['dp'=4,'seq'=4,'tensor'=2] {'dp','seq'}, use_global_device_ids=true, to_apply=%add.9 | all-reduce | flops 768 | bytes 3072
  771.8 78.7 %reduce-scatter.11.cloned.1.call-done = f32[48,768]{1,0:T(8,128)} async-done(((f32[768,768]{1,0:T(8,128)}), f32[48,768]{1,0:T(8,128)}) %reduce-scatter.11.cloned.1.call-update) | async-done | bytes 147472 | tf_op jit(solution)/shard_map/reduce_scatter | solution.py:395
  853.0 124.5 %reduce-scatter.19.cloned.1.call-done = f32[48,12]{1,0:T(8,128)} async-done(((f32[768,12]{1,0:T(8,128)}), f32[48,12]{1,0:T(8,128)}) %reduce-scatter.19.cloned.1.call-update) | async-done | bytes 2320
  979.6 125.1 %reduce-scatter.15.cloned.1.call-done = f32[48,128]{1,0:T(8,128)} async-done(((f32[768,128]{1,0:T(8,128)}), f32[48,128]{1,0:T(8,128)}) %reduce-scatter.15.cloned.1.call-update) | async-done | bytes 24592 | tf_op jit(solution)/shard_map/reduce_scatter | solution.py:397
  1106.8 22.8 %all-reduce.17.cloned.1.call-done = f32[2,256,768]{2,1,0:T(8,128)} async-done(((f32[2,256,768]{2,1,0:T(8,128)}), f32[2,256,768]{2,1,0:T(8,128)}) %all-reduce.17.cloned.1.call-update) | async-done | bytes 1572880 | tf_op jit(solution)/shard_map/psum | solution.py:378
  1131.7 56.3 %all-reduce.11 = (f32[768]{0:T(1024)S(1)}, f32[768]{0:T(1024)S(1)}, f32[5,768]{1,0:T(8,128)S(1)}, f32[5,128]{1,0:T(8,128)S(1)}, f32[3,12]{1,0:T(4,128)S(1)}) all-reduce(f32[768]{0:T(1024)S(1)} %get-tuple-element.440, f32[768]{0:T(1024)S(1)} %copy-done.108, ...), channel_id=11, replica_groups=mesh['dp'=4,'seq'=4,'tensor'=2] {'dp','seq'}, use_global_device_ids=true, to_apply=%region_31.32.clone | all-reduce | flops 6052 | bytes 48416
  1195.9 66.6 %reduce-scatter.13.cloned.1.call-done = f32[48,768]{1,0:T(8,128)} async-done(((f32[768,768]{1,0:T(8,128)}), f32[48,768]{1,0:T(8,128)}) %reduce-scatter.13.cloned.1.call-update) | async-done | bytes 147472 | tf_op jit(solution)/shard_map/reduce_scatter | solution.py:396
  (483 shorter events, 213.2 us)
Async XLA Ops:
  7.2 109.2 %all-gather.14.cloned.1.call-start = ((), (), s32[]{:S(2)}) async-start(), calls=%async_computation.6 | async-start | bytes 1253376 | tf_op jit(solution)/shard_map/all_gather | solution.py:211
  8.9 159.2 %all-gather.16.cloned.1.call-start = ((), (), s32[]{:S(2)}) async-start(), calls=%async_computation.7 | async-start | bytes 1253376 | tf_op jit(solution)/shard_map/all_gather | solution.py:210
  75.0 40.4 %collective-permute-start.1 = (bf16[2,3,128]{2,1,0:T(4,128)(2,1)S(1)}, bf16[2,3,128]{2,1,0:T(4,128)(2,1)S(1)}, u32[]{:S(2)}, u32[]{:S(2)}) collective-permute-start(bf16[2,3,128]{2,1,0:T(4,128)(2,1)S(1)} %slice.255), channel_id=1, source_target_pairs={{0,2},{2,4},{4,6},{1,3},{3,5},{5,7},{8,10},{10,12},{12,14},{9,11},... | collective-permute-start | bytes 4616 | tf_op jit(solution)/shard_map/ppermute | solution.py:24
  80.2 136.7 %all-gather.26.cloned.1.call-start = ((), (), s32[]{:S(2)}) async-start(), calls=%async_computation.19 | async-start | bytes 3932160 | tf_op jit(solution)/shard_map/all_gather | solution.py:29
  118.5 29.0 %collective-permute-start = (bf16[2,3,768]{2,1,0:T(4,128)(2,1)S(1)}, bf16[2,3,768]{2,1,0:T(4,128)(2,1)S(1)}, u32[]{:S(2)}, u32[]{:S(2)}) collective-permute-start(bf16[2,3,768]{2,1,0:T(4,128)(2,1)S(1)} %slice.250), channel_id=1, source_target_pairs={{0,2},{2,4},{4,6},{1,3},{3,5},{5,7},{8,10},{10,12},{12,14},{9,11},... | collective-permute-start | bytes 27656 | tf_op jit(solution)/shard_map/ppermute | solution.py:24
  154.4 210.8 %reduce-scatter.17.cloned.1.call-start = ((), (), s32[]{:S(2)}) async-start(), calls=%async_computation.18 | async-start | bytes 2506752 | tf_op jit(solution)/shard_map/reduce_scatter | solution.py:399
  237.4 185.1 %all-gather.18.cloned.1.call-start = ((), (), s32[]{:S(2)}) async-start(), calls=%async_computation.8 | async-start | bytes 1253376 | tf_op jit(solution)/shard_map/all_gather | solution.py:214
  367.0 82.7 %all-reduce.15.cloned.1.call-start = ((), (), s32[]{:S(2)}) async-start(), calls=%async_computation.9 | async-start | bytes 3145728 | tf_op jit(solution)/shard_map/psum | solution.py:285
  427.1 79.8 %all-gather.20.cloned.1.call-start = ((), (), s32[]{:S(2)}) async-start(), calls=%async_computation.10 | async-start | bytes 1253376 | tf_op jit(solution)/shard_map/all_gather | solution.py:295
  452.5 137.4 %all-gather.28.cloned.1.call-start = ((), (), s32[]{:S(2)}) async-start(), calls=%async_computation.20 | async-start | bytes 3932160 | tf_op jit(solution)/shard_map/all_gather | solution.py:29
  529.4 148.1 %all-gather.22.cloned.1.call-start = ((), (), s32[]{:S(2)}) async-start(), calls=%async_computation.11 | async-start | bytes 1253376 | tf_op jit(solution)/shard_map/all_gather | solution.py:291
  530.2 189.2 %reduce-scatter.9.cloned.1.call-start = ((), (), s32[]{:S(2)}) async-start(), calls=%async_computation.13 | async-start | bytes 786432 | tf_op jit(solution)/shard_map/reduce_scatter | solution.py:351
  603.5 127.2 %all-gather.24.cloned.1.call-start = ((), (), s32[]{:S(2)}) async-start(), calls=%async_computation.12 | async-start | bytes 1253376 | tf_op jit(solution)/shard_map/all_gather | solution.py:292
  604.3 246.3 %reduce-scatter.11.cloned.1.call-start = ((), (), s32[]{:S(2)}) async-start(), calls=%async_computation.15 | async-start | bytes 2506752 | tf_op jit(solution)/shard_map/reduce_scatter | solution.py:395
  642.3 335.2 %reduce-scatter.19.cloned.1.call-start = ((), (), s32[]{:S(2)}) async-start(), calls=%async_computation.21 | async-start | bytes 417792
  710.2 8.3 collective-permute-start.2
  718.2 386.6 %reduce-scatter.15.cloned.1.call-start = ((), (), s32[]{:S(2)}) async-start(), calls=%async_computation.17 | async-start | bytes 417792 | tf_op jit(solution)/shard_map/reduce_scatter | solution.py:397
  720.8 6.1 collective-permute-start.3
  728.2 401.3 %all-reduce.17.cloned.1.call-start = ((), (), s32[]{:S(2)}) async-start(), calls=%async_computation.14 | async-start | bytes 3145728 | tf_op jit(solution)/shard_map/psum | solution.py:378
  735.1 527.4 %reduce-scatter.13.cloned.1.call-start = ((), (), s32[]{:S(2)}) async-start(), calls=%async_computation.16 | async-start | bytes 2506752 | tf_op jit(solution)/shard_map/reduce_scatter | solution.py:396
  738.8 366.0 %copy-start.50 = (f32[48,128]{1,0:T(8,128)S(1)}, f32[48,128]{1,0:T(8,128)}, u32[]{:S(2)}) copy-start(f32[48,128]{1,0:T(8,128)} %param.30) | copy-start | bytes 73732
  738.8 366.0 %copy-start.58 = (f32[2,48,128]{2,1,0:T(8,128)S(1)}, f32[2,48,128]{2,1,0:T(8,128)}, u32[]{:S(2)}) copy-start(f32[2,48,128]{2,1,0:T(8,128)} %param.40) | copy-start | bytes 147460
  738.8 390.8 %copy-start.11 = (bf16[2,256,768]{2,1,0:T(8,128)(2,1)S(1)}, bf16[2,256,768]{2,1,0:T(8,128)(2,1)}, u32[]{:S(2)}) copy-start(bf16[2,256,768]{2,1,0:T(8,128)(2,1)} %param.26) | copy-start | bytes 2359300
  738.8 390.8 %copy-start.68 = (f32[2,256]{1,0:T(2,128)S(1)}, f32[2,256]{1,0:T(2,128)}, u32[]{:S(2)}) copy-start(f32[2,256]{1,0:T(2,128)} %copy-done.67) | copy-start | bytes 6148
  (118 other events, 4180.0 us)
Sparse Core Ops, SparseCore 0:
  10.8 55.1 all-gather.13
  80.4 68.4 all-gather.15
  154.5 62.3 all-gather.25
  237.5 127.6 reduce-scatter.16
  368.4 54.0 all-gather.17
  427.2 22.4 all-reduce.14
  453.1 53.7 all-gather.19
  529.6 60.3 all-gather.27
  593.3 54.8 all-gather.21
  650.3 9.8 reduce-scatter.8
  663.0 53.7 all-gather.23
  722.1 128.3 reduce-scatter.10
  855.2 122.2 reduce-scatter.18
  982.6 122.1 reduce-scatter.14
  1107.5 21.9 all-reduce.16
  1134.9 127.5 reduce-scatter.12
where the time goes:
time: 1280 us; the launch traced here: 1270 us
  waiting for transfers between devices  765 us (60%)
  blocking collectives  276 us (22%)
  matrix products  72.8 us (6%)
  other arithmetic  64.5 us (5%)
  local copies, waits for them, and re-layouts  62.1 us (5%)
  between operations  17.3 us (1%)
  starting transfers between devices  14.5 us (1%)
    reduce_scatter x1, waiting for transfers between devices, shards(): lax.psum_scatter(output_grad, ('dp', 'seq'), scatter_dimension=1, tiled=T...  128 us
    unnamed x17, waiting for transfers between devices  126 us
    reduce_scatter x1, waiting for transfers between devices, shards(): lax.psum_scatter(selector_grad, ('dp', 'seq'), scatter_dimension=0, tiled...  125 us
    unnamed x3, blocking collectives  115 us
    all_gather x2, waiting for transfers between devices, carried_in(): pieces = jax.tree.map(lambda part: lax.all_gather(part, axis), value)  89.5 us
    reduce_scatter x1, waiting for transfers between devices, shards(): lax.psum_scatter(gating_grad, ('dp', 'seq'), scatter_dimension=0, tiled=T...  78.7 us
    reduce_scatter x1, waiting for transfers between devices, shards(): lax.psum_scatter(values_grad, ('dp', 'seq'), scatter_dimension=0, tiled=T...  66.6 us
    all_gather x1, waiting for transfers between devices, shards(): lax.all_gather(late[4], ('dp', 'seq'), axis=1, tiled=True)  53.5 us
  transfers between devices with their start and end apart: 20, of which 12 were waited for; matrix products, arithmetic and copies ran while one was open for 12% of the time, Pallas kernels for 0%

commit v1 on v0

v1 whole, which is shorter than its diff:
```python
import functools
import jax
import jax.numpy as jnp
from jax import lax
from jax.experimental import pallas as pl
from jax.experimental.pallas import tpu as pltpu
from jax.sharding import PartitionSpec as P

INNER = 1536
STATE = 128
HEADDIM = 64
STEP = 2


epsilon = 1e-05
highest = lax.Precision.HIGHEST
learn_rate = 0.01
first_decay = 0.9
second_decay = 0.999
adam_epsilon = 1e-08
weight_decay = 0.1


def from_behind(block, axis, distance):
    devices = range(lax.axis_size(axis))
    route = [(i - distance, i) for i in devices if i - distance in devices]
    return lax.ppermute(block, axis, route)


MESH = pl.DeviceIdType.MESH
VMEM = pl.BlockSpec(memory_space=pltpu.VMEM)
ANY = pl.BlockSpec(memory_space=pl.ANY)


def send(src, dst, send_sem, recv_sem, device):
    return pltpu.make_async_remote_copy(
        src_ref=src,
        dst_ref=dst,
        send_sem=send_sem,
        recv_sem=recv_sem,
        device_id=device,
        device_id_type=MESH,
    )


def greet(devices):
    barrier = pltpu.get_barrier_semaphore()
    for device in devices:
        pl.semaphore_signal(barrier, inc=1, device_id=device, device_id_type=MESH)
    pl.semaphore_wait(barrier, len(devices))


def params_of(collective_id):
    return pltpu.CompilerParams(collective_id=collective_id, has_side_effects=True)


def swap_kernel(x_ref, o_ref, send_sem, recv_sem):
    other = {"tensor": 1 - lax.axis_index("tensor")}
    greet([other])
    copy = send(x_ref, o_ref, send_sem, recv_sem, other)
    copy.start()
    copy.wait()


def swap(value, collective_id):
    return pl.pallas_call(
        swap_kernel,
        out_shape=jax.ShapeDtypeStruct(value.shape, value.dtype),
        in_specs=[VMEM],
        out_specs=VMEM,
        scratch_shapes=[pltpu.SemaphoreType.DMA, pltpu.SemaphoreType.DMA],
        compiler_params=params_of(collective_id),
    )(value)


def carry_kernel(count, step, parts, decay_ref, local_ref, o_ref, out_buf, in_buf, send_sem, recv_sem):
    me = lax.axis_index("seq")
    target = lax.rem(me + count + step, count)
    source = lax.rem(me + count - step, count)
    first, last = (0, count - 1) if step > 0 else (count - 1, 0)
    greet([{"seq": target}, {"seq": source}])
    size = local_ref.shape[0] // parts

    def copy_of(part):
        return send(
            out_buf.at[part],
            in_buf.at[part],
            send_sem.at[part],
            recv_sem.at[part],
            {"seq": target},
        )

    for part in range(parts):
        rows = pl.ds(part * size, size)

        @pl.when(me == first)
        def _():
            o_ref[rows] = jnp.zeros((size,) + o_ref.shape[1:], o_ref.dtype)
            out_buf[part] = local_ref[rows].astype(jnp.bfloat16)

        @pl.when(me != first)
        def _():
            copy_of(part).wait_recv()
            entering = in_buf[part]
            o_ref[rows] = entering
            out_buf[part] = (
                decay_ref[rows] * entering.astype(jnp.float32) + local_ref[rows]
            ).astype(jnp.bfloat16)

        @pl.when(me != last)
        def _():
            copy_of(part).start()

    @pl.when(me != last)
    def _():
        for part in range(parts):
            copy_of(part).wait_send()


def carry(decay, local, count, step, collective_id):
    seqs, heads, wide, deep = local.shape
    total = seqs * heads
    parts = 6 if total % 6 == 0 else 1
    size = total // parts
    spread = jnp.broadcast_to(decay.reshape(total, 1, 1), (total, 1, deep))
    result = pl.pallas_call(
        functools.partial(carry_kernel, count, step, parts),
        out_shape=jax.ShapeDtypeStruct((total, wide, deep), jnp.bfloat16),
        in_specs=[VMEM, VMEM],
        out_specs=VMEM,
        scratch_shapes=[
            pltpu.VMEM((parts, size, wide, deep), jnp.bfloat16),
            pltpu.VMEM((parts, size, wide, deep), jnp.bfloat16),
            pltpu.SemaphoreType.DMA((parts,)),
            pltpu.SemaphoreType.DMA((parts,)),
        ],
        compiler_params=params_of(collective_id),
    )(spread, local.reshape(total, wide, deep))
    return result.reshape(local.shape)


def gather_kernel(n, x_ref, o_ref, own_sem, zs, zr, xs, xr, ys, yr, fxs, fxr, fys, fyr):
    d, s = lax.axis_index("dp"), lax.axis_index("seq")
    y, x = d // 2, lax.rem(d, 2)
    xn, yn = y * 2 + (1 - x), (1 - y) * 2 + x
    zt = [lax.rem(s + k, n) for k in range(n)]
    zf = [lax.rem(s + n - k, n) for k in range(n)]
    greet([{"seq": zt[k]} for k in range(1, n)] + [{"dp": xn}, {"dp": yn}])
    h = x_ref.shape[1] // 2
    own = pltpu.make_async_copy(x_ref, o_ref.at[d, s], own_sem)
    own.start()
    pend, xc, yc, fx, fy = [], [], [], [], []
    zc = []
    for k in range(1, n):
        copy = send(x_ref, o_ref.at[d, s], zs.at[k - 1], zr.at[k - 1], {"seq": zt[k]})
        zc.append(copy)

    def forward(j):
        z = zf[j]
        xc[j].wait_recv()
        copy = send(
            o_ref.at[xn, z, :, pl.ds(0, h)],
            o_ref.at[xn, z, :, pl.ds(0, h)],
            fys.at[j],
            fyr.at[j],
            {"dp": yn},
        )
        copy.start()
        fy.append(copy)
        yc[j].wait_recv()
        copy = send(
            o_ref.at[yn, z, :, pl.ds(h, h)],
            o_ref.at[yn, z, :, pl.ds(h, h)],
            fxs.at[j],
            fxr.at[j],
            {"dp": xn},
        )
        copy.start()
        fx.append(copy)

    for j in range(n):
        z = zf[j]
        if j:
            zc[j - 1].wait_recv()
        block = x_ref if j == 0 else o_ref.at[d, z]
        copy = send(block, o_ref.at[d, z], xs.at[j], xr.at[j], {"dp": xn})
        copy.start()
        xc.append(copy)
        copy = send(block, o_ref.at[d, z], ys.at[j], yr.at[j], {"dp": yn})
        copy.start()
        yc.append(copy)
        if j == 0:
            for copy in zc:
                copy.start()
        else:
            forward(j - 1)
    forward(n - 1)
    for copy in fx + fy:
        copy.wait_recv()
    for copy in zc + xc + yc + fx + fy:
        copy.wait_send()
    own.wait()


def gather(packed, n):
    rows, columns = packed.shape
    dma = pltpu.SemaphoreType.DMA
    return pl.pallas_call(
        functools.partial(gather_kernel, n),
        out_shape=jax.ShapeDtypeStruct((4, n, rows, columns), packed.dtype),
        in_specs=[VMEM],
        out_specs=ANY,
        scratch_shapes=[dma, dma((n - 1,)), dma((n - 1,))] + [dma((n,))] * 8,
        compiler_params=params_of(0),
    )(packed).reshape(4 * n * rows, columns)


def reduce_kernel(
    n, g_ref, small_ref, o_ref, small_o,
    rxa, rya, ryb, rxb, ta, tb, zb, zin, zsmall, dsmall,
    s1, r1, s2, r2, s3, r3, s4, r4, s5, r5, s6, r6, s7, r7,
):
    d, s = lax.axis_index("dp"), lax.axis_index("seq")
    y, x = d // 2, lax.rem(d, 2)
    xn, yn = {"dp": y * 2 + (1 - x)}, {"dp": (1 - y) * 2 + x}
    zt = [lax.rem(s + k, n) for k in range(n)]
    others = [{"dp": lax.rem(d + k, 4)} for k in range(1, 4)]
    greet([{"seq": zt[k]} for k in range(1, n)] + others)
    h = g_ref.shape[4] // 2
    left, right = pl.ds(0, h), pl.ds(h, h)
    single, half = jnp.float32, jnp.bfloat16
    order = list(range(1, n)) + [0]
    smalls = []
    for k in range(1, n):
        copy = send(small_ref, zsmall.at[s], s6.at[k - 1], r6.at[k - 1], {"seq": zt[k]})
        copy.start()
        smalls.append(copy)
    a1, b1, a2, b2, z1 = {}, {}, {}, {}, {}
    for j in order:
        a1[j] = send(g_ref.at[:, 1 - x, zt[j], :, left], rxa.at[j], s1.at[j], r1.at[j], xn)
        a1[j].start()
        b1[j] = send(g_ref.at[1 - y, :, zt[j], :, right], ryb.at[j], s2.at[j], r2.at[j], yn)
        b1[j].start()
    zsmall[s] = small_ref[...]
    for copy in smalls:
        copy.wait_recv()
    total = zsmall[0]
    for k in range(1, n):
        total = total + zsmall[k]
    dsmall[d] = total
    widely = []
    for k in range(3):
        copy = send(dsmall.at[d], dsmall.at[d], s7.at[k], r7.at[k], others[k])
        copy.start()
        widely.append(copy)

    def middle(j):
        z = zt[j]
        a1[j].wait_recv()
        ta[j] = (
            g_ref[1 - y, x, z, :, left].astype(single) + rxa[j, 1 - y].astype(single)
        ).astype(half)
        a2[j] = send(ta.at[j], rya.at[j], s3.at[j], r3.at[j], yn)
        a2[j].start()
        b1[j].wait_recv()
        tb[j] = (
            g_ref[y, 1 - x, z, :, right].astype(single) + ryb[j, 1 - x].astype(single)
        ).astype(half)
        b2[j] = send(tb.at[j], rxb.at[j], s4.at[j], r4.at[j], xn)
        b2[j].start()

    def finish(j):
        z = zt[j]
        a2[j].wait_recv()
        low = (
            g_ref[y, x, z, :, left].astype(single)
            + rxa[j, y].astype(single)
            + rya[j].astype(single)
        )
        b2[j].wait_recv()
        high = (
            g_ref[y, x, z, :, right].astype(single)
            + ryb[j, x].astype(single)
            + rxb[j].astype(single)
        )
        if j == 0:
            o_ref[:, left] = low
            o_ref[:, right] = high
        else:
            zb[j - 1, :, left] = low.astype(half)
            zb[j - 1, :, right] = high.astype(half)
            z1[j] = send(
                zb.at[j - 1], zin.at[j - 1], s5.at[j - 1], r5.at[j - 1], {"seq": zt[j]}
            )
            z1[j].start()

    for place, j in enumerate(order):
        middle(j)
        if place:
            finish(order[place - 1])
    finish(0)
    for copy in widely:
        copy.wait_recv()
    small_o[...] = dsmall[0] + dsmall[1] + dsmall[2] + dsmall[3]
    for j in range(1, n):
        z1[j].wait_recv()
        o_ref[...] = o_ref[...] + zin[j - 1].astype(single)
    for copy in smalls + widely:
        copy.wait_send()
    for group in (a1, b1, a2, b2, z1):
        for copy in group.values():
            copy.wait_send()


def reduce(grads, small, n):
    rows, columns = grads.shape[0] // (4 * n), grads.shape[1]
    h = columns // 2
    half = jnp.bfloat16
    dma = pltpu.SemaphoreType.DMA
    block = pltpu.VMEM((n, rows, h), half)
    double = pltpu.VMEM((n, 2, rows, h), half)
    row = pltpu.VMEM((n - 1, rows, columns), half)
    sems = [dma((n,))] * 8 + [dma((n - 1,))] * 4 + [dma((3,))] * 2
    return pl.pallas_call(
        functools.partial(reduce_kernel, n),
        out_shape=(
            jax.ShapeDtypeStruct((rows, columns), jnp.float32),
            jax.ShapeDtypeStruct(small.shape, jnp.float32),
        ),
        in_specs=[VMEM, VMEM],
        out_specs=(VMEM, VMEM),
        scratch_shapes=[double, block, double, block, block, block, row, row]
        + [
            pltpu.VMEM((n,) + small.shape, jnp.float32),
            pltpu.VMEM((4,) + small.shape, jnp.float32),
        ]
        + sems,
        compiler_params=params_of(9),
    )(grads.reshape(2, 2, n, rows, columns), small)


def swish_parts(value):
    sigmoid = jax.nn.sigmoid(value)
    return (value * sigmoid, sigmoid * (1.0 + value * (1.0 - sigmoid)))


def conv_apply(padded, taps):
    tap_count = taps.shape[0] - 1
    length = padded.shape[1] - tap_count + 1
    wide = padded.astype(jnp.float32)
    total = taps[tap_count] + taps[0] * wide[:, 0:length]
    for index in range(1, tap_count):
        total = total + taps[index] * wide[:, index : index + length]
    return total


def conv_back(padded, taps, grad_pre):
    tap_count = taps.shape[0] - 1
    length = grad_pre.shape[1]
    wide = padded.astype(jnp.float32)
    tap_rows = [
        jnp.sum(grad_pre * wide[:, index : index + length], axis=(0, 1))
        for index in range(tap_count)
    ]
    tap_rows.append(jnp.sum(grad_pre, axis=(0, 1)))
    grad_pad = jnp.zeros(padded.shape, jnp.float32)
    for index in range(tap_count):
        grad_pad = grad_pad + jnp.pad(
            taps[index] * grad_pre, ((0, 0), (index, tap_count - 1 - index), (0, 0))
        )
    return (jnp.stack(tap_rows), grad_pad)


def adamw(param, moments, grad):
    first = first_decay * moments[0] + (1.0 - first_decay) * grad
    second = second_decay * moments[1] + (1.0 - second_decay) * grad * grad
    first_hat = first / (1.0 - first_decay**STEP)
    second_hat = second / (1.0 - second_decay**STEP)
    fresh = param - learn_rate * (
        first_hat / (jnp.sqrt(second_hat) + adam_epsilon) + weight_decay * param
    )
    return (fresh, jnp.stack([first, second]))


def shards(
    hidden,
    cotangent,
    gating,
    values,
    selector,
    timestep,
    output,
    prenorm,
    postnorm,
    filters,
    kernels,
    scalars,
    gating_adam,
    values_adam,
    selector_adam,
    timestep_adam,
    output_adam,
    prenorm_adam,
    postnorm_adam,
    filters_adam,
    kernels_adam,
    scalars_adam,
):
    half = jnp.bfloat16
    single = jnp.float32
    n_dp, n_seq = lax.axis_size("dp"), lax.axis_size("seq")
    core = lax.axis_index("tensor")
    seqs_dev, length, width = hidden.shape
    rows = seqs_dev * length
    own_rows = gating.shape[0]
    lead = filters.shape[0] - 2
    heads_here = timestep.shape[1]
    inner_here = gating.shape[1]
    select_here = selector.shape[1]
    conv_end = 2 * inner_here + select_here
    step_wide = 128
    in_wide = conv_end + step_wide
    packed = jnp.concatenate(
        [
            gating.astype(half),
            values.astype(half),
            selector.astype(half),
            timestep.astype(half),
            prenorm.astype(half)[:, None],
            jnp.zeros((own_rows, step_wide - heads_here - 1), half),
            output.T.astype(half),
        ],
        axis=1,
    )
    if n_dp == 4:
        weights = gather(packed, n_seq)
    else:
        weights = lax.all_gather(packed, ("dp", "seq"), axis=0, tiled=True)
    in_weight = weights[:, :in_wide]
    out_weight = weights[:, in_wide:]
    bias = scalars[0]
    rate = -jnp.exp(scalars[1])
    skip = scalars[2]
    entry_gain = weights[:, conv_end + heads_here].astype(single)
    residual = hidden.astype(single)
    entry_scale = lax.rsqrt(jnp.mean(residual * residual, axis=-1, keepdims=True) + epsilon)
    normed = (residual * entry_scale * entry_gain).astype(half)
    flat = normed.reshape(rows, width)
    raw = jnp.dot(flat, in_weight, preferred_element_type=single)
    gate_raw = raw[:, :inner_here].astype(half).reshape(seqs_dev, length, inner_here)
    conv_raw = raw[:, inner_here:conv_end].astype(half).reshape(seqs_dev, length, -1)
    delta_raw = raw[:, conv_end : conv_end + heads_here].reshape(seqs_dev, length, heads_here)
    tails = from_behind(conv_raw[:, length - lead :], "seq", 1)
    conv_pad = jnp.concatenate([tails, conv_raw], axis=1)
    taps = jnp.concatenate([filters, kernels], axis=1)
    conv_value, conv_slope = swish_parts(conv_apply(conv_pad, taps))
    conv_act = conv_value.astype(half)
    inner_act = conv_act[:, :, :inner_here]
    mine = conv_act[:, :, inner_here:]
    theirs = swap(mine.reshape(rows, select_here), 1).reshape(mine.shape)
    write_vec = jnp.where(core == 0, mine, theirs)
    read_vec = jnp.where(core == 0, theirs, mine)
    delta = jax.nn.softplus(delta_raw + bias)
    running = jnp.cumsum(delta * rate, axis=1)
    inner_h = inner_act.reshape(seqs_dev, length, heads_here, HEADDIM)
    inner_f = inner_h.astype(single)
    weight_end = jnp.exp(running[:, -1:, :] - running) * delta
    carry_decay = jnp.exp(running[:, -1, :])
    growth = jnp.exp(running)
    inner_w = (inner_f * weight_end[..., None]).astype(half)
    local_state = jnp.einsum("bthp,btn->bhpn", inner_w, write_vec, preferred_element_type=single)
    entering = carry(carry_decay, local_state, n_seq, 1, 7)
    scores = jnp.einsum("btn,bun->btu", read_vec, write_vec, preferred_element_type=single)
    causal = jnp.arange(length)[:, None] >= jnp.arange(length)[None, :]
    by_head = jnp.transpose(running, (0, 2, 1))
    gap = by_head[:, :, :, None] - by_head[:, :, None, :]
    decays = jnp.exp(jnp.where(causal, gap, -jnp.inf))
    step_head = jnp.transpose(delta, (0, 2, 1))
    mixing_b = (scores[:, None] * decays * step_head[:, :, None, :]).astype(half)
    within = jnp.einsum("bhtu,buhp->bthp", mixing_b, inner_h, preferred_element_type=single)
    across = jnp.einsum("btn,bhpn->bthp", read_vec, entering, preferred_element_type=single)
    mixer_out = (within + growth[..., None] * across + skip[None, None, :, None] * inner_f).reshape(
        seqs_dev, length, inner_here
    )
    gate_act, gate_slope = swish_parts(gate_raw.astype(single))
    gated = mixer_out * gate_act
    upstream = cotangent.reshape(rows, width)
    grad_mixed = jnp.dot(upstream, out_weight, preferred_element_type=single).reshape(
        seqs_dev, length, inner_here
    )
    hat_gated = grad_mixed * postnorm
    sums = jnp.stack([jnp.sum(gated * gated, axis=-1), jnp.sum(hat_gated * gated, axis=-1)])
    lanes = sums.reshape(-1, 128)
    sums = (lanes + swap(lanes, 2)).reshape(sums.shape)
    squares, dots = sums[0], sums[1]
    gate_scale = lax.rsqrt(squares / INNER + epsilon)[..., None]
    mixed_flat = (gated * gate_scale * postnorm).astype(half).reshape(rows, inner_here)
    branch = lax.dot_general(
        mixed_flat, out_weight, (((1,), (1,)), ((), ())), preferred_element_type=single
    ).astype(half)
    branch = branch.astype(single) + swap(branch, 3).astype(single)
    result = residual + branch.reshape(seqs_dev, length, width)
    output_grad = lax.dot_general(
        upstream, mixed_flat, (((0,), (0,)), ((), ())), preferred_element_type=single
    )
    postnorm_grad = jnp.sum(grad_mixed * gated * gate_scale, axis=(0, 1))
    cube = gate_scale * gate_scale * gate_scale
    grad_gated = gate_scale * hat_gated - gated * cube * (dots / INNER)[..., None]
    grad_mixer = (grad_gated * gate_act).reshape(seqs_dev, length, heads_here, HEADDIM)
    grad_gate = (grad_gated * mixer_out * gate_slope).astype(half).reshape(rows, inner_here)

    scaled = (grad_mixer * growth[..., None]).astype(half)
    pushed = jnp.einsum("bthp,btn->bhpn", scaled, read_vec, preferred_element_type=single)
    end_grad = carry(carry_decay, pushed, n_seq, -1, 8)

    grad_half = grad_mixer.astype(half)
    skip_grad = jnp.sum(grad_mixer * inner_f, axis=(0, 1, 3))
    grad_inner = skip[None, None, :, None] * grad_mixer + jnp.einsum(
        "bhtu,bthp->buhp", mixing_b, grad_half, preferred_element_type=single
    )
    grad_mix = jnp.einsum("bthp,buhp->bhtu", grad_half, inner_h, preferred_element_type=single)
    spread_mix = grad_mix * decays
    kernel = spread_mix * scores[:, None]
    grad_delta = jnp.transpose(jnp.sum(kernel, axis=2), (0, 2, 1))
    weighted = kernel * step_head[:, :, None, :]
    grad_running = jnp.transpose(jnp.sum(weighted, axis=3) - jnp.sum(weighted, axis=2), (0, 2, 1))
    grad_scores = jnp.sum(spread_mix * step_head[:, :, None, :], axis=1).astype(half)
    grad_read = jnp.einsum("btu,bun->btn", grad_scores, write_vec, preferred_element_type=single)
    grad_write = jnp.einsum("btu,btn->bun", grad_scores, read_vec, preferred_element_type=single)
    grad_running = grad_running + jnp.sum(grad_mixer * across, axis=3) * growth
    grad_read = grad_read + jnp.einsum(
        "bthp,bhpn->btn", scaled, entering, preferred_element_type=single
    )

    decay_grad = jnp.sum(end_grad.astype(single) * entering.astype(single), axis=(2, 3))
    end_extra = decay_grad * carry_decay
    grad_xw = jnp.einsum("bhpn,btn->bthp", end_grad, write_vec, preferred_element_type=single)
    grad_write = grad_write + jnp.einsum(
        "bhpn,bthp->btn", end_grad, inner_w, preferred_element_type=single
    )
    grad_inner = grad_inner + grad_xw * weight_end[..., None]
    grad_weight = jnp.sum(grad_xw * inner_f, axis=3)
    grad_delta = grad_delta + grad_weight * jnp.exp(running[:, -1:, :] - running)
    spread = grad_weight * weight_end
    end_extra = end_extra + jnp.sum(spread, axis=1)
    grad_running = grad_running - spread
    grad_running = jnp.concatenate(
        [grad_running[:, :-1], grad_running[:, -1:] + end_extra[:, None]], axis=1
    )
    grad_log = jnp.flip(jnp.cumsum(jnp.flip(grad_running, 1), axis=1), 1)

    grad_delta = grad_delta + grad_log * rate
    alog_grad = jnp.sum(grad_log * delta, axis=(0, 1)) * rate
    grad_delta_pre = grad_delta * jax.nn.sigmoid(delta_raw + bias)
    bias_grad = jnp.sum(grad_delta_pre, axis=(0, 1))
    kept = jnp.where(core == 0, grad_write, grad_read)
    given = jnp.where(core == 0, grad_read, grad_write)
    grad_select = kept + swap(given.reshape(rows, select_here), 4).reshape(kept.shape)
    grad_conv = jnp.concatenate(
        [grad_inner.reshape(seqs_dev, length, inner_here), grad_select], axis=2
    )
    taps_grad, conv_pad_grad = conv_back(conv_pad, taps, grad_conv * conv_slope)
    back = from_behind(conv_pad_grad[:, :lead], "seq", -1)
    conv_raw_grad = (
        jnp.concatenate(
            [conv_pad_grad[:, lead:length], conv_pad_grad[:, length:] + back], axis=1
        )
        .astype(half)
        .reshape(rows, -1)
    )
    grad_all = jnp.concatenate(
        [
            grad_gate,
            conv_raw_grad,
            grad_delta_pre.astype(half).reshape(rows, heads_here),
            jnp.zeros((rows, step_wide - heads_here), half),
        ],
        axis=1,
    )
    grad_part = lax.dot_general(
        grad_all, in_weight, (((1,), (1,)), ((), ())), preferred_element_type=single
    ).astype(half)
    grad_part = grad_part.astype(single) + swap(grad_part, 5).astype(single)
    grad_normed = grad_part.reshape(seqs_dev, length, width)
    in_grad = lax.dot_general(
        flat, grad_all, (((0,), (0,)), ((), ())), preferred_element_type=single
    )
    prenorm_grad = jnp.sum(grad_normed * residual * entry_scale, axis=(0, 1))
    hat = grad_normed * entry_gain
    hidden_grad = (
        cotangent.astype(single)
        + entry_scale * hat
        - residual
        * entry_scale
        * entry_scale
        * entry_scale
        * jnp.mean(hat * residual, axis=-1, keepdims=True)
    )
    gain_column = conv_end + heads_here
    packed_grad = jnp.concatenate(
        [
            in_grad[:, :gain_column].astype(half),
            prenorm_grad.astype(half)[:, None],
            in_grad[:, gain_column + 1 :].astype(half),
            output_grad.astype(half),
        ],
        axis=1,
    )
    tap_rows = filters.shape[0]
    scalars_local = jnp.stack([bias_grad, alog_grad, skip_grad])
    loose = jnp.concatenate([taps_grad[:, inner_here:].reshape(-1), scalars_local.reshape(-1)])
    small = jnp.concatenate(
        [
            taps_grad[:, :inner_here],
            postnorm_grad[None],
            jnp.pad(loose, (0, inner_here - loose.shape[0]))[None],
            jnp.zeros((8 - tap_rows - 2, inner_here), single),
        ],
        axis=0,
    )
    if n_dp == 4:
        summed, small = reduce(packed_grad, small, n_seq)
    else:
        summed = lax.psum_scatter(
            packed_grad.astype(single), ("dp", "seq"), scatter_dimension=0, tiled=True
        )
        small = lax.psum(small, ("dp", "seq"))
    loose_end = tap_rows * select_here
    grads = (
        summed[:, :inner_here],
        summed[:, inner_here : 2 * inner_here],
        summed[:, 2 * inner_here : conv_end],
        summed[:, conv_end:gain_column],
        summed[:, in_wide:].T,
        summed[:, gain_column],
        small[tap_rows],
        small[:tap_rows],
        small[tap_rows + 1, :loose_end].reshape(tap_rows, select_here),
        small[tap_rows + 1, loose_end : loose_end + 3 * heads_here].reshape(3, heads_here),
    )
    params = (
        gating,
        values,
        selector,
        timestep,
        output,
        prenorm,
        postnorm,
        filters,
        kernels,
        scalars,
    )
    moments = (
        gating_adam,
        values_adam,
        selector_adam,
        timestep_adam,
        output_adam,
        prenorm_adam,
        postnorm_adam,
        filters_adam,
        kernels_adam,
        scalars_adam,
    )
    updated = [adamw(param, moment, grad) for param, moment, grad in zip(params, moments, grads)]
    return (
        result,
        hidden_grad,
        grads[0],
        grads[1],
        grads[2],
        grads[3],
        grads[4],
        grads[5],
        grads[6],
        grads[7],
        grads[8],
        grads[9],
        updated[0][0],
        updated[1][0],
        updated[2][0],
        updated[3][0],
        updated[4][0],
        updated[5][0],
        updated[6][0],
        updated[7][0],
        updated[8][0],
        updated[9][0],
        updated[0][1],
        updated[1][1],
        updated[2][1],
        updated[3][1],
        updated[4][1],
        updated[5][1],
        updated[6][1],
        updated[7][1],
        updated[8][1],
        updated[9][1],
    )


def solution(mesh):
    placed = (
        P("dp", "seq", None),
        P("dp", "seq", None),
        P(("dp", "seq"), "tensor"),
        P(("dp", "seq"), "tensor"),
        P(("dp", "seq"), "tensor"),
        P(("dp", "seq"), "tensor"),
        P("tensor", ("dp", "seq")),
        P(("dp", "seq")),
        P("tensor"),
        P(None, "tensor"),
        P(None, "tensor"),
        P(None, "tensor"),
        P(None, ("dp", "seq"), "tensor"),
        P(None, ("dp", "seq"), "tensor"),
        P(None, ("dp", "seq"), "tensor"),
        P(None, ("dp", "seq"), "tensor"),
        P(None, "tensor", ("dp", "seq")),
        P(None, ("dp", "seq")),
        P(None, "tensor"),
        P(None, None, "tensor"),
        P(None, None, "tensor"),
        P(None, None, "tensor"),
    )
    return jax.shard_map(
        shards,
        mesh=mesh,
        in_specs=placed,
        out_specs=(
            P("dp", "seq", None),
            P("dp", "seq", None),
            P(("dp", "seq"), "tensor"),
            P(("dp", "seq"), "tensor"),
            P(("dp", "seq"), "tensor"),
            P(("dp", "seq"), "tensor"),
            P("tensor", ("dp", "seq")),
            P(("dp", "seq")),
            P("tensor"),
            P(None, "tensor"),
            P(None, "tensor"),
            P(None, "tensor"),
            P(("dp", "seq"), "tensor"),
            P(("dp", "seq"), "tensor"),
            P(("dp", "seq"), "tensor"),
            P(("dp", "seq"), "tensor"),
            P("tensor", ("dp", "seq")),
            P(("dp", "seq")),
            P("tensor"),
            P(None, "tensor"),
            P(None, "tensor"),
            P(None, "tensor"),
            P(None, ("dp", "seq"), "tensor"),
            P(None, ("dp", "seq"), "tensor"),
            P(None, ("dp", "seq"), "tensor"),
            P(None, ("dp", "seq"), "tensor"),
            P(None, "tensor", ("dp", "seq")),
            P(None, ("dp", "seq")),
            P(None, "tensor"),
            P(None, None, "tensor"),
            P(None, None, "tensor"),
            P(None, None, "tensor"),
        ),
        check_vma=False,
    )
```

time: 1280 us -> 365 us (0.29)
  waiting for transfers between devices: 765 us -> 0.01 us
  blocking collectives: 276 us -> 0 us
  Pallas kernels: 0 us -> 159 us
  matrix products: 72.8 us -> 47.3 us
  other arithmetic: 64.5 us -> 80.8 us
  between operations: 17.3 us -> 2.28 us
    reduce_scatter x5 -> x0, waiting for transfers between devices: 398 us -> none  [the longest x1 128 us: shards(): lax.psum_scatter(output_grad, ('dp', 'seq'), scatter_dimension=1, tiled=T...]
    all_gather x8 -> x0, waiting for transfers between devices: 192 us -> none  [the longest x2 89.5 us: carried_in(): pieces = jax.tree.map(lambda part: lax.all_gather(part, axis), value)]
    pallas_call x0 -> x9, Pallas kernels: none -> 159 us  [the longest x1 54.8 us: reduce(): pl.pallas_call(functools.partial(reduce_kernel, n), out_shape=(jax.ShapeD...]
    all_gather x6 -> x0, blocking collectives: 154 us -> none  [the longest x1 33.2 us: shards(): lax.all_gather(select_half, ('dp', 'seq'), axis=0, tiled=True)]
    unnamed x17 -> x0, waiting for transfers between devices: 126 us -> none
    unnamed x3 -> x0, blocking collectives: 115 us -> none
    psum x2 -> x0, waiting for transfers between devices: 44.8 us -> none  [the longest x1 22.8 us: shards(): grad_normed = lax.psum(grad_part, 'tensor').reshape(seqs_dev, length, width)]
    dot_general x27 -> x18, matrix products: 72.8 us -> 47.3 us  [the longest x1 5.16 us: shards(): jnp.einsum('bthp,buhp->bhtu', grad_half, inner_h, preferred_element_type=...]
  transfers between devices with their start and end apart: 20 -> 2, of which waited for: 12 -> 0; matrix products, arithmetic and copies ran while one was open for 12% -> 13% of each run, Pallas kernels for 0% -> 1%
where the time goes in v1:
time: 365 us; the launch traced here: 362 us
  Pallas kernels  159 us (44%)
  other arithmetic  80.8 us (22%)
  local copies, waits for them, and re-layouts  66.1 us (18%)
  matrix products  47.3 us (13%)
  starting transfers between devices  6.4 us (2%)
    pallas_call x1, Pallas kernels, reduce(): pl.pallas_call(functools.partial(reduce_kernel, n), out_shape=(jax.ShapeD...  54.8 us
    pallas_call x2, Pallas kernels, carry(): pl.pallas_call(functools.partial(carry_kernel, count, step, parts), out_s...  40.1 us
    pallas_call x1, Pallas kernels, gather(): pl.pallas_call(functools.partial(gather_kernel, n), out_shape=jax.ShapeDt...  39 us
    pallas_call x5, Pallas kernels, swap(): pl.pallas_call(swap_kernel, out_shape=jax.ShapeDtypeStruct(value.shape, v...  25.3 us
    another operation x19, other arithmetic, adamw(): return (fresh, jnp.stack([first, second]))  20.6 us
    unnamed x254, local copies, waits for them, and re-layouts  13.3 us
  transfers between devices with their start and end apart: 2, of which 0 were waited for; matrix products, arithmetic and copies ran while one was open for 13% of the time, Pallas kernels for 1%

profile of v1, /device:TPU:11, one launch (start us, length us, event | category | flops | bytes accessed | tf_op | source)
XLA Modules:
  0.0 362.0 jit_solution(10711614506506471218)
XLA Ops:
  8.0 39.0 %shard_map.461 = bf16[4,4,48,2560]{3,2,1,0:T(8,128)(2,1)} custom-call(bf16[48,2560]{1,0:T(8,128)(2,1)} %concatenate.39.x_ref), custom_call_target="tpu_custom_call" | custom-call | tf_op jit(solution)/shard_map/pallas_call | solution.py:208
  48.8 3.7 %fusion.124 = (bf16[512,1792]{1,0:T(8,128)(2,1)S(1)}, f32[512,1792]{1,0:T(8,128)S(1)}) fusion(bf16[512,768]{1,0:T(8,128)(2,1)S(1)} %bitcast.315, bf16[768,2560]{1,0:T(8,128)(2,1)} %bitcast.293), kind=kOutput, calls=%fused_computation.284 | convolution fusion | flops 1410203648 | bytes 9043968 | tf_op jit(solution)/shard_map/dot_general | solution.py:449
  73.9 8.1 %shard_map.462 = bf16[512,128]{1,0:T(8,128)(2,1)} custom-call(bf16[512,128]{1,0:T(8,128)(2,1)} %bitcast.329), custom_call_target="tpu_custom_call" | custom-call | tf_op jit(solution)/shard_map/pallas_call | solution.py:66
  85.7 17.7 %shard_map.463 = bf16[24,64,128]{2,1,0:T(8,128)(2,1)} custom-call(f32[24,1,128]{2,1,0:T(1,128)} %broadcast_in_dim.26.decay_ref, f32[24,64,128]{2,1,0:T(8,128)} %bitcast.318), custom_call_target="tpu_custom_call" | custom-call | tf_op jit(solution)/shard_map/pallas_call | solution.py:126
  112.3 5.0 %multiply_reduce_fusion.10 = (f32[512]{0:T(512)}, f32[512,768]{1,0:T(8,128)}) fusion(f32[768]{0:T(1024)} %param.30, f32[512,768]{1,0:T(8,128)S(1)} %copy.255, bf16[512,1792]{1,0:T(8,128)(2,1)} %copy-done.12, bf16[512,768]{1,0:T(8,128)(2,1)} %bitcast.326, bf16[768,2560]{1,0:T(8,128)(2,1)} %bitcast.294), kind=kOutput, calls=%fused_computation.63 | convolution fusion | flops 607518208 | bytes 5904384 | tf_op jit(solution)/shard_map/dot_general | solution.py:488
  119.3 3.9 %shard_map.464 = f32[8,128]{1,0:T(8,128)} custom-call(f32[8,128]{1,0:T(8,128)} %reshape.459.x_ref), custom_call_target="tpu_custom_call" | custom-call | tf_op jit(solution)/shard_map/pallas_call | solution.py:66
  131.7 3.1 fusion.24
  136.1 5.2 %multiply_reduce_fusion.1 = (f32[2,12,256]{2,1,0:T(8,128)}, f32[2,12,256]{2,1,0:T(8,128)}, f32[2,12,256]{2,1,0:T(8,128)}, bf16[2,256,256]{2,1,0:T(8,128)(2,1)}) fusion(f32[2,12,256]{2,1,0:T(8,128)S(1)} %copy-done.82, f32[2,256,256]{2,1,0:T(8,128)S(1)} %copy-done.51, f32[2,12,256]{2,1,0:T(8,128)S(1)} %reshape.485, pred[256,256]{1,0:T(8,128)(4,1)S(1)} %copy-done.71, ...), kind=kOutput, calls=%fused_computation.4 | convolution fusion | flops 217298944 | bytes 3334144 | tf_op jit(solution)/shard_map/bthp,buhp->bhtu/dot_general | solution.py:521
  142.4 22.4 %shard_map.466 = bf16[24,64,128]{2,1,0:T(8,128)(2,1)} custom-call(f32[24,1,128]{2,1,0:T(1,128)} %broadcast_in_dim.26.decay_ref, f32[24,64,128]{2,1,0:T(8,128)} %bitcast.317), custom_call_target="tpu_custom_call" | custom-call | tf_op jit(solution)/shard_map/pallas_call | solution.py:126
  166.7 3.9 %fusion.16 = (f32[12]{0:T(128)}, f32[2,256,12]{1,2,0:T(8,128)}, f32[2,256,12]{1,2,0:T(8,128)}, f32[2,256,12,64]{1,3,2,0:T(8,128)}) fusion(f32[2,256,12,64]{1,3,2,0:T(8,128)S(1)} %fusion.24, bf16[2,256,12,64]{1,3,2,0:T(8,128)(2,1)S(1)} %bitcast.301, f32[2,256,12,64]{1,3,2,0:T(8,128)} %copy-done.21, bf16[2,12,64,128]{3,2,1,0:T(8,128)(2,1)S(1)} %bitcast.313, ...), kind=kOutput, calls=%fused_computation.43 | convolution fusion | flops 103403504 | bytes 6078512 | tf_op jit(solution)/shard_map/bhpn,btn->bthp/dot_general | solution.py:537
  172.7 4.3 %shard_map.467 = f32[512,128]{1,0:T(8,128)} custom-call(f32[512,128]{1,0:T(8,128)} %bitcast.323), custom_call_target="tpu_custom_call" | custom-call | tf_op jit(solution)/shard_map/pallas_call | solution.py:66
  177.1 4.9 %fusion.21 = f32[2,256,12,64]{1,3,2,0:T(8,128)} fusion(f32[2,256,12,64]{1,3,2,0:T(8,128)} %get-tuple-element.302, f32[2,256,12,64]{1,3,2,0:T(8,128)S(1)} %fusion.24, f32[2,12,256]{2,1,0:T(8,128)} %get-tuple-element.263, f32[2,12,256]{2,1,0:T(8,128)S(1)} %reshape.485, f32[2,256,256]{2,1,0:T(8,128)} %copy-done.50, pred[256,256]{1,0:T(8,128)(4,1)} %iota_compare_fusion, ...), kind=kOutput, calls=%fused_computation.49 | convolution fusion | flops 211156992 | bytes 5382192 | tf_op jit(solution)/shard_map/bhtu,bthp->buhp/dot_general | solution.py:518
  184.9 3.6 multiply_reduce_fusion.4
  193.9 4.3 %collective-permute-start.1 = (f32[2,3,896]{2,1,0:T(4,128)}, f32[2,3,896]{2,1,0:T(4,128)}, u32[]{:S(2)}, u32[]{:S(2)}) collective-permute-start(f32[2,3,896]{2,1,0:T(4,128)} %pad_add_fusion.1), channel_id=1, source_target_pairs={{2,0},{4,2},{6,4},{3,1},{5,3},{7,5},{10,8},{12,10},{14,12},{11,9},... | collective-permute-start | bytes 64520 | tf_op jit(solution)/shard_map/ppermute | solution.py:27
  205.7 3.1 reduce-window.16
  212.7 3.6 convolution_convert_fusion.1.x_ref
  216.3 4.6 %shard_map.465 = bf16[512,768]{1,0:T(8,128)(2,1)} custom-call(bf16[512,768]{1,0:T(8,128)(2,1)} %convolution_convert_fusion.1.x_ref), custom_call_target="tpu_custom_call" | custom-call | tf_op jit(solution)/shard_map/pallas_call | solution.py:66
  227.9 3.0 multiply_reduce_fusion.8
  240.2 4.4 %fusion.25.x_ref = bf16[512,768]{1,0:T(8,128)(2,1)} fusion(bf16[512,1792]{1,0:T(8,128)(2,1)S(1)} %concatenate.44, bf16[768,2560]{1,0:T(8,128)(2,1)} %bitcast.296), kind=kOutput, calls=%fused_computation.70 | convolution fusion | flops 1409679360 | bytes 5373952 | tf_op jit(solution)/shard_map/dot_general | solution.py:580
  244.5 3.2 convolution_convert_fusion
  247.7 4.4 %shard_map.468 = bf16[512,768]{1,0:T(8,128)(2,1)} custom-call(bf16[512,768]{1,0:T(8,128)(2,1)} %fusion.25.x_ref), custom_call_target="tpu_custom_call" | custom-call | tf_op jit(solution)/shard_map/pallas_call | solution.py:66
  258.5 6.5 %concatenate.48.g_ref = bf16[2,2,4,48,2560]{4,3,2,1,0:T(8,128)(2,1)} concatenate(bf16[2,2,4,48,1676]{4,3,2,1,0:T(8,128)(2,1)} %bitcast.314, bf16[2,2,4,48,1]{4,3,2,1,0:T(8,128)(2,1)} %convert_element_type.207, bf16[2,2,4,48,115]{4,3,2,1,0:T(8,128)(2,1)} %bitcast.327, bf16[2,2,4,48,768]{4,3,2,1,0:T(8,128)(2,1)S(1)} %bitcast.320), dimensions={4} | concatenate | bytes 7864320 | tf_op jit(solution)/shard_map/concatenate | solution.py:600
  265.1 54.8 %shard_map.469 = (f32[48,2560]{1,0:T(8,128)}, f32[8,768]{1,0:T(8,128)}) custom-call(bf16[2,2,4,48,2560]{4,3,2,1,0:T(8,128)(2,1)} %concatenate.48.g_ref, f32[8,768]{1,0:T(8,128)} %maximum_maximum_fusion.small_ref), custom_call_target="tpu_custom_call" | custom-call | tf_op jit(solution)/shard_map/pallas_call | solution.py:324
  353.4 4.0 %fusion.12 = (f32[2,256,768]{2,1,0:T(8,128)}, f32[2,256,768]{2,1,0:T(8,128)}) fusion(bf16[2,256,768]{2,1,0:T(8,128)(2,1)S(1)} %copy-done.9, bf16[2,256,768]{2,1,0:T(8,128)(2,1)S(1)} %copy-done.40, f32[2,256]{1,0:T(2,128)} %broadcast_multiply_fusion.4, f32[768]{0:T(1024)} %copy-done.68, f32[2,256]{1,0:T(2,128)} %copy-done.79, ...), kind=kLoop, calls=%fused_computation.39 | loop fusion | flops 5505024 | bytes 7871488 | tf_op jit(solution)/shard_map/sub | solution.py:591
  (417 shorter events, 139.1 us)
Async XLA Ops:
  2.0 46.1 %copy-start.79 = (f32[2,256]{1,0:T(2,128)}, f32[2,256]{1,0:T(2,128)S(1)}, u32[]{:S(2)}) copy-start(f32[2,256]{1,0:T(2,128)S(1)} %add_rsqrt_fusion.1) | copy-start | bytes 6148
  8.0 40.2 %copy-start.8 = (bf16[2,256,768]{2,1,0:T(8,128)(2,1)S(1)}, bf16[2,256,768]{2,1,0:T(8,128)(2,1)}, u32[]{:S(2)}) copy-start(bf16[2,256,768]{2,1,0:T(8,128)(2,1)} %param.22) | copy-start | bytes 2359300
  52.7 15.5 %collective-permute-start = (bf16[2,3,896]{2,1,0:T(4,128)(2,1)S(1)}, bf16[2,3,896]{2,1,0:T(4,128)(2,1)S(1)}, u32[]{:S(2)}, u32[]{:S(2)}) collective-permute-start(bf16[2,3,896]{2,1,0:T(4,128)(2,1)S(1)} %slice.290), channel_id=1, source_target_pairs={{0,2},{2,4},{4,6},{1,3},{3,5},{5,7},{8,10},{10,12},{12,14},{9,11},... | collective-permute-start | bytes 32264 | tf_op jit(solution)/shard_map/ppermute | solution.py:27
  73.9 31.0 %copy-start.13 = (bf16[2,256,768]{1,2,0:T(8,128)(2,1)}, bf16[2,256,768]{1,2,0:T(8,128)(2,1)S(1)}, u32[]{:S(2)}) copy-start(bf16[2,256,768]{1,2,0:T(8,128)(2,1)S(1)} %copy.246) | copy-start | bytes 2359300
  83.1 20.4 %copy-start.27 = (bf16[2,256,128]{2,1,0:T(8,128)(2,1)}, bf16[2,256,128]{2,1,0:T(8,128)(2,1)S(1)}, u32[]{:S(2)}) copy-start(bf16[2,256,128]{2,1,0:T(8,128)(2,1)S(1)} %get-tuple-element.240) | copy-start | bytes 393220
  83.3 21.6 %copy-start.50 = (f32[2,256,256]{2,1,0:T(8,128)}, f32[2,256,256]{2,1,0:T(8,128)S(1)}, u32[]{:S(2)}) copy-start(f32[2,256,256]{2,1,0:T(8,128)S(1)} %fusion.125) | copy-start | bytes 1572868
  85.7 19.3 %copy-start.81 = (f32[2,12,256]{2,1,0:T(8,128)S(1)}, f32[2,12,256]{2,1,0:T(8,128)}, u32[]{:S(2)}) copy-start(f32[2,12,256]{2,1,0:T(8,128)} %get-tuple-element.263) | copy-start | bytes 73732
  191.4 21.3 %copy-start.19 = (f32[512,768]{1,0:T(8,128)S(1)}, f32[512,768]{1,0:T(8,128)}, u32[]{:S(2)}) copy-start(f32[512,768]{1,0:T(8,128)} %copy-done.18) | copy-start | bytes 4718596
  191.4 21.3 %copy-start.75 = (f32[768]{0:T(1024)S(1)}, f32[768]{0:T(1024)}, u32[]{:S(2)}) copy-start(f32[768]{0:T(1024)} %param.30) | copy-start | bytes 9220
  193.9 42.7 %collective-permute-start.1 = (f32[2,3,896]{2,1,0:T(4,128)}, f32[2,3,896]{2,1,0:T(4,128)}, u32[]{:S(2)}, u32[]{:S(2)}) collective-permute-start(f32[2,3,896]{2,1,0:T(4,128)} %pad_add_fusion.1), channel_id=1, source_target_pairs={{2,0},{4,2},{6,4},{3,1},{5,3},{7,5},{10,8},{12,10},{14,12},{11,9},... | collective-permute-start | bytes 64520 | tf_op jit(solution)/shard_map/ppermute | solution.py:27
  265.0 57.8 %copy-start.111 = (f32[2,48]{1,0:T(2,128)S(1)}, f32[2,48]{1,0:T(2,128)}, u32[]{:S(2)}) copy-start(f32[2,48]{1,0:T(2,128)} %param.39) | copy-start | bytes 1156
  265.0 57.8 %copy-start.118 = (f32[48]{0:T(128)S(1)}, f32[48]{0:T(128)}, u32[]{:S(2)}) copy-start(f32[48]{0:T(128)} %param.29) | copy-start | bytes 580
  265.0 58.9 %copy-start.87 = (f32[1,5,128]{2,0,1:T(1,128)S(1)}, f32[1,5,128]{2,0,1:T(1,128)}, u32[]{:S(2)}) copy-start(f32[1,5,128]{2,0,1:T(1,128)} %get-tuple-element.277) | copy-start | bytes 7684
  265.0 58.9 %copy-start.88 = (f32[1,5,128]{2,0,1:T(1,128)S(1)}, f32[1,5,128]{2,0,1:T(1,128)}, u32[]{:S(2)}) copy-start(f32[1,5,128]{2,0,1:T(1,128)} %get-tuple-element.278) | copy-start | bytes 7684
  265.0 58.9 %copy-start.95 = (f32[5,128]{1,0:T(8,128)S(1)}, f32[5,128]{1,0:T(8,128)}, u32[]{:S(2)}) copy-start(f32[5,128]{1,0:T(8,128)} %param.32) | copy-start | bytes 7684
  265.0 60.1 %copy-start.102 = (f32[2,256]{1,0:T(2,128)S(1)}, f32[2,256]{1,0:T(2,128)}, u32[]{:S(2)}) copy-start(f32[2,256]{1,0:T(2,128)} %get-tuple-element.209) | copy-start | bytes 6148
  265.0 60.7 %copy-start.59 = (f32[2,48,128]{2,1,0:T(8,128)S(1)}, f32[2,48,128]{2,1,0:T(8,128)}, u32[]{:S(2)}) copy-start(f32[2,48,128]{2,1,0:T(8,128)} %param.36) | copy-start | bytes 147460
  265.0 62.1 %copy-start.61 = (f32[48,12]{1,0:T(8,128)S(1)}, f32[48,12]{1,0:T(8,128)}, u32[]{:S(2)}) copy-start(f32[48,12]{1,0:T(8,128)} %copy.281) | copy-start | bytes 6916
  265.1 62.0 %copy-start.62 = (f32[1,48,12]{2,1,0:T(8,128)S(1)}, f32[1,48,12]{2,1,0:T(8,128)}, u32[]{:S(2)}) copy-start(f32[1,48,12]{2,1,0:T(8,128)} %copy.316) | copy-start | bytes 6916
  265.1 62.0 %copy-start.63 = (f32[1,48,12]{2,1,0:T(8,128)S(1)}, f32[1,48,12]{2,1,0:T(8,128)}, u32[]{:S(2)}) copy-start(f32[1,48,12]{2,1,0:T(8,128)} %copy.317) | copy-start | bytes 6916
  265.1 64.1 %copy-start.43 = (f32[2,768,48]{1,2,0:T(8,128)S(1)}, f32[2,768,48]{1,2,0:T(8,128)}, u32[]{:S(2)}) copy-start(f32[2,768,48]{1,2,0:T(8,128)} %param.38) | copy-start | bytes 884740
  265.1 65.7 %copy-start.106 = (f32[2,768]{1,0:T(2,128)S(1)}, f32[2,768]{1,0:T(2,128)}, u32[]{:S(2)}) copy-start(f32[2,768]{1,0:T(2,128)} %param.40) | copy-start | bytes 18436
  265.1 69.7 %copy-start.41 = (f32[2,48,768]{2,1,0:T(8,128)S(1)}, f32[2,48,768]{2,1,0:T(8,128)}, u32[]{:S(2)}) copy-start(f32[2,48,768]{2,1,0:T(8,128)} %param.34) | copy-start | bytes 884740
  265.1 69.7 %copy-start.42 = (f32[2,48,768]{2,1,0:T(8,128)S(1)}, f32[2,48,768]{2,1,0:T(8,128)}, u32[]{:S(2)}) copy-start(f32[2,48,768]{2,1,0:T(8,128)} %param.35) | copy-start | bytes 884740
  (100 other events, 454.8 us)

commit v2 on v1

--- a/solution.py
+++ b/solution.py
@@ -216,17 +216,23 @@
 
 
 def reduce_kernel(
-    n, g_ref, small_ref, o_ref, small_o,
-    rxa, rya, ryb, rxb, ta, tb, zb, zin, zsmall, dsmall,
+    n, g_ref, small_ref, u_ref, v_ref, o_ref, small_o, uo, vo,
+    rxa, rya, ryb, rxb, ta, tb, zb, zin, zsmall, dsmall, tsmall, cs, cr,
     s1, r1, s2, r2, s3, r3, s4, r4, s5, r5, s6, r6, s7, r7,
 ):
     d, s = lax.axis_index("dp"), lax.axis_index("seq")
     y, x = d // 2, lax.rem(d, 2)
     xn, yn = {"dp": y * 2 + (1 - x)}, {"dp": (1 - y) * 2 + x}
     zt = [lax.rem(s + k, n) for k in range(n)]
+    core = {"tensor": 1 - lax.axis_index("tensor")}
     others = [{"dp": lax.rem(d + k, 4)} for k in range(1, 4)]
-    greet([{"seq": zt[k]} for k in range(1, n)] + others)
+    greet([{"seq": zt[k]} for k in range(1, n)] + others + [core])
     h = g_ref.shape[4] // 2
+    cores = [
+        send(u_ref, uo, cs.at[0], cr.at[0], core),
+        send(v_ref, vo, cs.at[1], cr.at[1], core),
+        send(dsmall.at[4], tsmall, cs.at[2], cr.at[2], core),
+    ]
     left, right = pl.ds(0, h), pl.ds(h, h)
     single, half = jnp.float32, jnp.bfloat16
     order = list(range(1, n)) + [0]
@@ -241,6 +247,8 @@
         a1[j].start()
         b1[j] = send(g_ref.at[1 - y, :, zt[j], :, right], ryb.at[j], s2.at[j], r2.at[j], yn)
         b1[j].start()
+    cores[0].start()
+    cores[1].start()
     zsmall[s] = small_ref[...]
     for copy in smalls:
         copy.wait_recv()
@@ -301,10 +309,17 @@
     finish(0)
     for copy in widely:
         copy.wait_recv()
-    small_o[...] = dsmall[0] + dsmall[1] + dsmall[2] + dsmall[3]
+    total = dsmall[0] + dsmall[1] + dsmall[2] + dsmall[3]
+    dsmall[4] = total
+    cores[2].start()
     for j in range(1, n):
         z1[j].wait_recv()
         o_ref[...] = o_ref[...] + zin[j - 1].astype(single)
+    for copy in cores:
+        copy.wait()
+    edge = small_ref.shape[0] - 1
+    small_o[...] = total
+    small_o[edge:] = dsmall[4, edge:] + tsmall[edge:]
     for copy in smalls + widely:
         copy.wait_send()
     for group in (a1, b1, a2, b2, z1):
@@ -312,7 +327,7 @@
             copy.wait_send()
 
 
-def reduce(grads, small, n):
+def reduce(grads, small, first, second, n):
     rows, columns = grads.shape[0] // (4 * n), grads.shape[1]
     h = columns // 2
     half = jnp.bfloat16
@@ -326,17 +341,22 @@
         out_shape=(
             jax.ShapeDtypeStruct((rows, columns), jnp.float32),
             jax.ShapeDtypeStruct(small.shape, jnp.float32),
+            jax.ShapeDtypeStruct(first.shape, first.dtype),
+            jax.ShapeDtypeStruct(second.shape, second.dtype),
         ),
-        in_specs=[VMEM, VMEM],
-        out_specs=(VMEM, VMEM),
+        in_specs=[VMEM] * 4,
+        out_specs=(VMEM,) * 4,
         scratch_shapes=[double, block, double, block, block, block, row, row]
         + [
             pltpu.VMEM((n,) + small.shape, jnp.float32),
-            pltpu.VMEM((4,) + small.shape, jnp.float32),
+            pltpu.VMEM((5,) + small.shape, jnp.float32),
+            pltpu.VMEM(small.shape, jnp.float32),
+            dma((3,)),
+            dma((3,)),
         ]
         + sems,
         compiler_params=params_of(9),
-    )(grads.reshape(2, 2, n, rows, columns), small)
+    )(grads.reshape(2, 2, n, rows, columns), small, first, second)
 
 
 def swish_parts(value):
@@ -498,8 +518,6 @@
     branch = lax.dot_general(
         mixed_flat, out_weight, (((1,), (1,)), ((), ())), preferred_element_type=single
     ).astype(half)
-    branch = branch.astype(single) + swap(branch, 3).astype(single)
-    result = residual + branch.reshape(seqs_dev, length, width)
     output_grad = lax.dot_general(
         upstream, mixed_flat, (((0,), (0,)), ((), ())), preferred_element_type=single
     )
@@ -580,12 +598,51 @@
     grad_part = lax.dot_general(
         grad_all, in_weight, (((1,), (1,)), ((), ())), preferred_element_type=single
     ).astype(half)
-    grad_part = grad_part.astype(single) + swap(grad_part, 5).astype(single)
-    grad_normed = grad_part.reshape(seqs_dev, length, width)
     in_grad = lax.dot_general(
         flat, grad_all, (((0,), (0,)), ((), ())), preferred_element_type=single
     )
-    prenorm_grad = jnp.sum(grad_normed * residual * entry_scale, axis=(0, 1))
+    prenorm_part = jnp.sum(
+        grad_part.astype(single).reshape(seqs_dev, length, width) * residual * entry_scale,
+        axis=(0, 1),
+    )
+    gain_column = conv_end + heads_here
+    packed_grad = jnp.concatenate(
+        [
+            in_grad.astype(half),
+            output_grad.astype(half),
+        ],
+        axis=1,
+    )
+    tap_rows = filters.shape[0]
+    scalars_local = jnp.stack([bias_grad, alog_grad, skip_grad])
+    loose = jnp.concatenate([taps_grad[:, inner_here:].reshape(-1), scalars_local.reshape(-1)])
+    small = jnp.concatenate(
+        [
+            taps_grad[:, :inner_here],
+            postnorm_grad[None],
+            jnp.pad(loose, (0, inner_here - loose.shape[0]))[None],
+            prenorm_part[None],
+        ],
+        axis=0,
+    )
+    if n_dp == 4:
+        summed, small, branch_far, part_far = reduce(
+            packed_grad, small, branch, grad_part, n_seq
+        )
+        prenorm_grad = small[-1]
+    else:
+        summed = lax.psum_scatter(
+            packed_grad.astype(single), ("dp", "seq"), scatter_dimension=0, tiled=True
+        )
+        small = lax.psum(small, ("dp", "seq"))
+        prenorm_grad = lax.psum(small[-1], "tensor")
+        branch_far, part_far = swap(branch, 3), swap(grad_part, 5)
+    own = lax.axis_index("dp") * n_seq + lax.axis_index("seq")
+    prenorm_grad = lax.dynamic_slice_in_dim(prenorm_grad, own * own_rows, own_rows)
+    branch = branch.astype(single) + branch_far.astype(single)
+    result = residual + branch.reshape(seqs_dev, length, width)
+    grad_part = grad_part.astype(single) + part_far.astype(single)
+    grad_normed = grad_part.reshape(seqs_dev, length, width)
     hat = grad_normed * entry_gain
     hidden_grad = (
         cotangent.astype(single)
@@ -596,35 +653,6 @@
         * entry_scale
         * jnp.mean(hat * residual, axis=-1, keepdims=True)
     )
-    gain_column = conv_end + heads_here
-    packed_grad = jnp.concatenate(
-        [
-            in_grad[:, :gain_column].astype(half),
-            prenorm_grad.astype(half)[:, None],
-            in_grad[:, gain_column + 1 :].astype(half),
-            output_grad.astype(half),
-        ],
-        axis=1,
-    )
-    tap_rows = filters.shape[0]
-    scalars_local = jnp.stack([bias_grad, alog_grad, skip_grad])
-    loose = jnp.concatenate([taps_grad[:, inner_here:].reshape(-1), scalars_local.reshape(-1)])
-    small = jnp.concatenate(
-        [
-            taps_grad[:, :inner_here],
-            postnorm_grad[None],
-            jnp.pad(loose, (0, inner_here - loose.shape[0]))[None],
-            jnp.zeros((8 - tap_rows - 2, inner_here), single),
-        ],
-        axis=0,
-    )
-    if n_dp == 4:
-        summed, small = reduce(packed_grad, small, n_seq)
-    else:
-        summed = lax.psum_scatter(
-            packed_grad.astype(single), ("dp", "seq"), scatter_dimension=0, tiled=True
-        )
-        small = lax.psum(small, ("dp", "seq"))
     loose_end = tap_rows * select_here
     grads = (
         summed[:, :inner_here],
@@ -632,7 +660,7 @@
         summed[:, 2 * inner_here : conv_end],
         summed[:, conv_end:gain_column],
         summed[:, in_wide:].T,
-        summed[:, gain_column],
+        prenorm_grad,
         small[tap_rows],
         small[:tap_rows],
         small[tap_rows + 1, :loose_end].reshape(tap_rows, select_here),

time: 365 us -> 328 us (0.90)
  other arithmetic: 80.8 us -> 65.6 us
  local copies, waits for them, and re-layouts: 66.1 us -> 54.5 us
  Pallas kernels: 159 us -> 151 us
    another operation x19, other arithmetic: 20.6 us -> 10.9 us  [adamw(): return (fresh, jnp.stack([first, second]))]
    pallas_call x5 -> x3, Pallas kernels: 25.3 us -> 16.1 us  [swap(): pl.pallas_call(swap_kernel, out_shape=jax.ShapeDtypeStruct(value.shape, v...]
    concatenate x2 -> x0, local copies, waits for them, and re-layouts: 7.03 us -> none  [the longest x1 6.45 us: shards(): jnp.concatenate([in_grad[:, :gain_column].astype(half), prenorm_grad.asty...]
    add x2 -> x1, other arithmetic: 4.19 us -> 0.4 us  [shards(): grad_part = grad_part.astype(single) + part_far.astype(single)]
    unnamed x254 -> x244, local copies, waits for them, and re-layouts: 13.3 us -> 12.2 us
  transfers between devices with their start and end apart: 2 -> 2, of which waited for: 0 -> 0; matrix products, arithmetic and copies ran while one was open for 13% -> 6% of each run, Pallas kernels for 1% -> 0%
where the time goes in v2:
time: 328 us; the launch traced here: 325 us
  Pallas kernels  151 us (46%)
  other arithmetic  65.6 us (20%)
  local copies, waits for them, and re-layouts  54.5 us (17%)
  matrix products  45.3 us (14%)
  starting transfers between devices  6.67 us (2%)
    pallas_call x1, Pallas kernels, reduce(): pl.pallas_call(functools.partial(reduce_kernel, n), out_shape=(jax.ShapeD...  55.5 us
    pallas_call x2, Pallas kernels, carry(): pl.pallas_call(functools.partial(carry_kernel, count, step, parts), out_s...  40 us
    pallas_call x1, Pallas kernels, gather(): pl.pallas_call(functools.partial(gather_kernel, n), out_shape=jax.ShapeDt...  39 us
    pallas_call x3, Pallas kernels, swap(): pl.pallas_call(swap_kernel, out_shape=jax.ShapeDtypeStruct(value.shape, v...  16.1 us
    unnamed x244, local copies, waits for them, and re-layouts  12.2 us
    another operation x19, other arithmetic, adamw(): return (fresh, jnp.stack([first, second]))  10.9 us
    ppermute x2, starting transfers between devices, from_behind(): return lax.ppermute(block, axis, route)  6.67 us
  transfers between devices with their start and end apart: 2, of which 0 were waited for; matrix products, arithmetic and copies ran while one was open for 6% of the time, Pallas kernels for 0%

profile of v2, /device:TPU:11, one launch (start us, length us, event | category | flops | bytes accessed | tf_op | source)
XLA Modules:
  0.0 324.9 jit_solution(11742787880913556847)
XLA Ops:
  8.0 39.0 %shard_map.461 = bf16[4,4,48,2560]{3,2,1,0:T(8,128)(2,1)} custom-call(bf16[48,2560]{1,0:T(8,128)(2,1)} %concatenate.32.x_ref), custom_call_target="tpu_custom_call" | custom-call | tf_op jit(solution)/shard_map/pallas_call | solution.py:208
  48.8 3.7 %fusion.128 = (bf16[512,1792]{1,0:T(8,128)(2,1)S(1)}, f32[512,1792]{1,0:T(8,128)S(1)}) fusion(bf16[512,768]{1,0:T(8,128)(2,1)S(1)} %bitcast.319, bf16[768,2560]{1,0:T(8,128)(2,1)} %bitcast.297), kind=kOutput, calls=%fused_computation.288 | convolution fusion | flops 1410203648 | bytes 9043968 | tf_op jit(solution)/shard_map/dot_general | solution.py:469
  69.8 2.4 multiply_convert_fusion.3
  73.2 7.9 %shard_map.462 = bf16[512,128]{1,0:T(8,128)(2,1)} custom-call(bf16[512,128]{1,0:T(8,128)(2,1)} %bitcast.331), custom_call_target="tpu_custom_call" | custom-call | tf_op jit(solution)/shard_map/pallas_call | solution.py:66
  86.1 17.7 %shard_map.463 = bf16[24,64,128]{2,1,0:T(8,128)(2,1)} custom-call(f32[24,1,128]{2,1,0:T(1,128)} %broadcast_in_dim.26.decay_ref, f32[24,64,128]{2,1,0:T(8,128)} %bitcast.322), custom_call_target="tpu_custom_call" | custom-call | tf_op jit(solution)/shard_map/pallas_call | solution.py:126
  105.4 3.0 multiply_reduce_fusion.11
  112.8 5.0 %multiply_reduce_fusion.10 = (f32[512]{0:T(512)}, f32[512,768]{1,0:T(8,128)}) fusion(f32[768]{0:T(1024)S(1)} %copy-done.68, f32[512,768]{1,0:T(8,128)S(1)} %copy.256, bf16[512,1792]{1,0:T(8,128)(2,1)} %copy-done.9, bf16[512,768]{1,0:T(8,128)(2,1)} %bitcast.329, bf16[768,2560]{1,0:T(8,128)(2,1)} %bitcast.298), kind=kOutput, calls=%fused_computation.67 | convolution fusion | flops 607518208 | bytes 5903360 | tf_op jit(solution)/shard_map/dot_general | solution.py:508
  119.8 3.9 %shard_map.464 = f32[8,128]{1,0:T(8,128)} custom-call(f32[8,128]{1,0:T(8,128)} %reshape.420.x_ref), custom_call_target="tpu_custom_call" | custom-call | tf_op jit(solution)/shard_map/pallas_call | solution.py:66
  130.9 3.1 fusion.27
  135.3 5.2 %multiply_reduce_fusion.1 = (f32[2,12,256]{2,1,0:T(8,128)}, f32[2,12,256]{2,1,0:T(8,128)}, f32[2,12,256]{2,1,0:T(8,128)}, bf16[2,256,256]{2,1,0:T(8,128)(2,1)}) fusion(f32[2,12,256]{2,1,0:T(8,128)S(1)} %copy-done.83, f32[2,256,256]{2,1,0:T(8,128)S(1)} %copy-done.48, f32[2,12,256]{2,1,0:T(8,128)S(1)} %reshape.448, pred[256,256]{1,0:T(8,128)(4,1)S(1)} %copy-done.67, ...), kind=kOutput, calls=%fused_computation.4 | convolution fusion | flops 217298944 | bytes 3334144 | tf_op jit(solution)/shard_map/bthp,buhp->bhtu/dot_general | solution.py:539
  141.7 22.3 %shard_map.465 = bf16[24,64,128]{2,1,0:T(8,128)(2,1)} custom-call(f32[24,1,128]{2,1,0:T(1,128)} %broadcast_in_dim.26.decay_ref, f32[24,64,128]{2,1,0:T(8,128)} %bitcast.321), custom_call_target="tpu_custom_call" | custom-call | tf_op jit(solution)/shard_map/pallas_call | solution.py:126
  165.9 4.3 %fusion.16 = (f32[12]{0:T(128)}, f32[2,256,12]{1,2,0:T(8,128)}, f32[2,256,12]{1,2,0:T(8,128)}, f32[2,256,12,64]{1,3,2,0:T(8,128)}) fusion(f32[2,256,12,64]{1,3,2,0:T(8,128)S(1)} %fusion.27, bf16[2,256,12,64]{1,3,2,0:T(8,128)(2,1)} %bitcast.305, f32[2,256,12,64]{1,3,2,0:T(8,128)} %copy-done.17, bf16[2,12,64,128]{3,2,1,0:T(8,128)(2,1)} %bitcast.317, ...), kind=kOutput, calls=%fused_computation.44 | convolution fusion | flops 103403504 | bytes 6078512 | tf_op jit(solution)/shard_map/bhpn,btn->bthp/dot_general | solution.py:555
  172.6 4.3 %shard_map.466 = f32[512,128]{1,0:T(8,128)} custom-call(f32[512,128]{1,0:T(8,128)} %bitcast.326), custom_call_target="tpu_custom_call" | custom-call | tf_op jit(solution)/shard_map/pallas_call | solution.py:66
  176.9 4.9 %fusion.24 = f32[2,256,12,64]{1,3,2,0:T(8,128)} fusion(f32[2,256,12,64]{1,3,2,0:T(8,128)} %get-tuple-element.307, f32[2,256,12,64]{1,3,2,0:T(8,128)S(1)} %fusion.27, f32[2,12,256]{2,1,0:T(8,128)} %get-tuple-element.267, f32[2,12,256]{2,1,0:T(8,128)S(1)} %reshape.448, f32[2,256,256]{2,1,0:T(8,128)} %copy-done.47, pred[256,256]{1,0:T(8,128)(4,1)} %iota_compare_fusion, ...), kind=kOutput, calls=%fused_computation.54 | convolution fusion | flops 211156992 | bytes 5382192 | tf_op jit(solution)/shard_map/bhtu,bthp->buhp/dot_general | solution.py:536
  184.8 3.4 %multiply_reduce_fusion.4 = (f32[896]{0:T(1024)}, f32[896]{0:T(1024)}, f32[896]{0:T(1024)}, f32[896]{0:T(1024)}, f32[896]{0:T(1024)}, /*index=5*/f32[2,256,896]{2,1,0:T(8,128)S(1)}) fusion(f32[2,259,896]{2,1,0:T(8,128)S(1)} %maximum_convert_fusion, f32[2,256,896]{2,1,0:T(8,128)} %get-tuple-element.237, f32[2,256,128]{2,1,0:T(8,128)S(1)} %select_add_fusion, ...), kind=kLoop, calls=%fused_computation.30 | loop fusion | flops 8253056 | bytes 12862976 | tf_op jit(solution)/shard_map/reduce_sum | solution.py:382
  196.3 3.6 %convolution_convert_fusion.1.u_ref = bf16[512,768]{1,0:T(8,128)(2,1)} fusion(bf16[768,2560]{1,0:T(8,128)(2,1)} %bitcast.299, f32[512]{0:T(512)S(1)} %copy-done.102, f32[768]{0:T(1024)S(1)} %copy-done.68, f32[512,768]{1,0:T(8,128)S(1)} %copy-done.14, bf16[512,1792]{1,0:T(8,128)(2,1)} %copy-done.9), kind=kOutput, calls=%fused_computation.74 | convolution fusion | flops 607911936 | bytes 4330496 | tf_op jit(solution)/shard_map/dot_general | solution.py:518
  211.0 3.1 reduce-window.16
  221.4 4.6 %collective-permute-start.1 = (f32[2,3,896]{2,1,0:T(4,128)}, f32[2,3,896]{2,1,0:T(4,128)S(1)}, u32[]{:S(2)}, u32[]{:S(2)}) collective-permute-start(f32[2,3,896]{2,1,0:T(4,128)} %pad_add_fusion.1), channel_id=1, source_target_pairs={{2,0},{4,2},{6,4},{3,1},{5,3},{7,5},{10,8},{12,10},{14,12},{11,9},... | collective-permute-start | bytes 64520 | tf_op jit(solution)/shard_map/ppermute | solution.py:27
  226.0 3.4 %multiply_reduce_fusion.8 = (f32[768]{0:T(1024)S(1)}, bf16[512,768]{1,0:T(8,128)(2,1)}) fusion(f32[512,768]{1,0:T(8,128)} %get-tuple-element.302, f32[512]{0:T(512)} %get-tuple-element.289, f32[512,768]{1,0:T(8,128)S(1)} %copy-done.14, bf16[512,1792]{1,0:T(8,128)(2,1)} %copy-done.9, f32[512]{0:T(512)} %get-tuple-element.290, ...), kind=kLoop, calls=%fused_computation.62 | loop fusion | flops 8256768 | bytes 4730880 | tf_op jit(solution)/shard_map/reduce_sum | solution.py:524
  234.8 2.4 concatenate.37
  237.2 4.4 %fusion.19 = (f32[768]{0:T(1024)S(1)}, bf16[512,768]{1,0:T(8,128)(2,1)}) fusion(bf16[2,256,768]{2,1,0:T(8,128)(2,1)S(1)} %copy-done.5, f32[2,256]{1,0:T(2,128)} %copy-done.78, bf16[512,1792]{1,0:T(8,128)(2,1)S(1)} %concatenate.37, bf16[768,2560]{1,0:T(8,128)(2,1)} %bitcast.300), kind=kOutput, calls=%fused_computation.47 | convolution fusion | flops 1411644672 | bytes 6165504 | tf_op jit(solution)/shard_map/dot_general | solution.py:598
  243.2 2.2 pad_maximum_fusion
  246.2 55.5 %shard_map.467 = (f32[48,2560]{1,0:T(8,128)}, f32[8,768]{1,0:T(8,128)}, bf16[512,768]{1,0:T(8,128)(2,1)}, bf16[512,768]{1,0:T(8,128)(2,1)}) custom-call(bf16[2,2,4,48,2560]{4,3,2,1,0:T(8,128)(2,1)} %bitcast.301, f32[8,768]{1,0:T(8,128)} %pad_maximum_fusion.8.small_ref, bf16[512,768]{1,0:T(8,128)(2,1)} %convolution_convert_fusion.1.u_ref, ...), custom_call_target="tpu_custom_call" | custom-call | tf_op jit(solution)/shard_map/pallas_call | solution.py:339
  321.0 2.4 fusion.12
  (402 shorter events, 111.1 us)
Async XLA Ops:
  2.7 45.5 %copy-start.78 = (f32[2,256]{1,0:T(2,128)}, f32[2,256]{1,0:T(2,128)S(1)}, u32[]{:S(2)}) copy-start(f32[2,256]{1,0:T(2,128)S(1)} %add_rsqrt_fusion.1) | copy-start | bytes 6148
  7.9 40.2 %copy-start.4 = (bf16[2,256,768]{2,1,0:T(8,128)(2,1)S(1)}, bf16[2,256,768]{2,1,0:T(8,128)(2,1)}, u32[]{:S(2)}) copy-start(bf16[2,256,768]{2,1,0:T(8,128)(2,1)} %param.22) | copy-start | bytes 2359300
  52.7 15.7 %collective-permute-start = (bf16[2,3,896]{2,1,0:T(4,128)(2,1)S(1)}, bf16[2,3,896]{2,1,0:T(4,128)(2,1)S(1)}, u32[]{:S(2)}, u32[]{:S(2)}) collective-permute-start(bf16[2,3,896]{2,1,0:T(4,128)(2,1)S(1)} %slice.280), channel_id=1, source_target_pairs={{0,2},{2,4},{4,6},{1,3},{3,5},{5,7},{8,10},{10,12},{12,14},{9,11},... | collective-permute-start | bytes 32264 | tf_op jit(solution)/shard_map/ppermute | solution.py:27
  81.4 23.9 %copy-start.10 = (bf16[2,256,768]{1,2,0:T(8,128)(2,1)}, bf16[2,256,768]{1,2,0:T(8,128)(2,1)S(1)}, u32[]{:S(2)}) copy-start(bf16[2,256,768]{1,2,0:T(8,128)(2,1)S(1)} %copy.247) | copy-start | bytes 2359300
  82.8 21.1 %copy-start.22 = (bf16[2,256,128]{2,1,0:T(8,128)(2,1)}, bf16[2,256,128]{2,1,0:T(8,128)(2,1)S(1)}, u32[]{:S(2)}) copy-start(bf16[2,256,128]{2,1,0:T(8,128)(2,1)S(1)} %get-tuple-element.244) | copy-start | bytes 393220
  83.0 22.4 %copy-start.47 = (f32[2,256,256]{2,1,0:T(8,128)}, f32[2,256,256]{2,1,0:T(8,128)S(1)}, u32[]{:S(2)}) copy-start(f32[2,256,256]{2,1,0:T(8,128)S(1)} %fusion.129) | copy-start | bytes 1572868
  221.4 11.5 %collective-permute-start.1 = (f32[2,3,896]{2,1,0:T(4,128)}, f32[2,3,896]{2,1,0:T(4,128)S(1)}, u32[]{:S(2)}, u32[]{:S(2)}) collective-permute-start(f32[2,3,896]{2,1,0:T(4,128)} %pad_add_fusion.1), channel_id=1, source_target_pairs={{2,0},{4,2},{6,4},{3,1},{5,3},{7,5},{10,8},{12,10},{14,12},{11,9},... | collective-permute-start | bytes 64520 | tf_op jit(solution)/shard_map/ppermute | solution.py:27
  246.1 57.3 %copy-start.86 = (f32[1,5,128]{2,0,1:T(1,128)S(1)}, f32[1,5,128]{2,0,1:T(1,128)}, u32[]{:S(2)}) copy-start(f32[1,5,128]{2,0,1:T(1,128)} %get-tuple-element.282) | copy-start | bytes 7684
  246.1 57.3 %copy-start.87 = (f32[1,5,128]{2,0,1:T(1,128)S(1)}, f32[1,5,128]{2,0,1:T(1,128)}, u32[]{:S(2)}) copy-start(f32[1,5,128]{2,0,1:T(1,128)} %get-tuple-element.283) | copy-start | bytes 7684
  246.1 57.3 %copy-start.95 = (f32[5,128]{1,0:T(8,128)S(1)}, f32[5,128]{1,0:T(8,128)}, u32[]{:S(2)}) copy-start(f32[5,128]{1,0:T(8,128)} %param.32) | copy-start | bytes 7684
  246.1 57.9 %copy-start.107 = (f32[2,768]{1,0:T(2,128)S(1)}, f32[2,768]{1,0:T(2,128)}, u32[]{:S(2)}) copy-start(f32[2,768]{1,0:T(2,128)} %param.40) | copy-start | bytes 18436
  246.1 58.8 %copy-start.110 = (f32[2,48]{1,0:T(2,128)S(1)}, f32[2,48]{1,0:T(2,128)}, u32[]{:S(2)}) copy-start(f32[2,48]{1,0:T(2,128)} %param.39) | copy-start | bytes 1156
  246.1 58.9 %copy-start.113 = (f32[48]{0:T(128)S(1)}, f32[48]{0:T(128)}, u32[]{:S(2)}) copy-start(f32[48]{0:T(128)} %param.29) | copy-start | bytes 580
  246.1 59.6 %copy-start.96 = (f32[1,3,12]{2,0,1:T(1,128)S(1)}, f32[1,3,12]{2,0,1:T(1,128)}, u32[]{:S(2)}) copy-start(f32[1,3,12]{2,0,1:T(1,128)} %get-tuple-element.292) | copy-start | bytes 436
  246.1 59.6 %copy-start.97 = (f32[1,3,12]{2,0,1:T(1,128)S(1)}, f32[1,3,12]{2,0,1:T(1,128)}, u32[]{:S(2)}) copy-start(f32[1,3,12]{2,0,1:T(1,128)} %get-tuple-element.293) | copy-start | bytes 436
  246.1 59.6 %copy-start.106 = (f32[3,12]{1,0:T(4,128)S(1)}, f32[3,12]{1,0:T(4,128)}, u32[]{:S(2)}) copy-start(f32[3,12]{1,0:T(4,128)} %param.33) | copy-start | bytes 436
  246.1 61.4 %copy-start.57 = (f32[48,12]{1,0:T(8,128)S(1)}, f32[48,12]{1,0:T(8,128)}, u32[]{:S(2)}) copy-start(f32[48,12]{1,0:T(8,128)} %copy.282) | copy-start | bytes 6916
  246.1 61.4 %copy-start.58 = (f32[1,48,12]{2,1,0:T(8,128)S(1)}, f32[1,48,12]{2,1,0:T(8,128)}, u32[]{:S(2)}) copy-start(f32[1,48,12]{2,1,0:T(8,128)} %copy.319) | copy-start | bytes 6916
  246.1 61.4 %copy-start.59 = (f32[1,48,12]{2,1,0:T(8,128)S(1)}, f32[1,48,12]{2,1,0:T(8,128)}, u32[]{:S(2)}) copy-start(f32[1,48,12]{2,1,0:T(8,128)} %copy.318) | copy-start | bytes 6916
  246.2 64.4 %copy-start.62 = (f32[5,768]{1,0:T(8,128)S(1)}, f32[5,768]{1,0:T(8,128)}, u32[]{:S(2)}) copy-start(f32[5,768]{1,0:T(8,128)} %param.31) | copy-start | bytes 46084
  246.2 64.4 %copy-start.70 = (f32[1,5,768]{2,0,1:T(1,128)S(1)}, f32[1,5,768]{2,0,1:T(1,128)}, u32[]{:S(2)}) copy-start(f32[1,5,768]{2,0,1:T(1,128)} %get-tuple-element.272) | copy-start | bytes 46084
  246.2 65.7 %copy-start.55 = (f32[2,48,128]{2,1,0:T(8,128)S(1)}, f32[2,48,128]{2,1,0:T(8,128)}, u32[]{:S(2)}) copy-start(f32[2,48,128]{2,1,0:T(8,128)} %param.36) | copy-start | bytes 147460
  246.2 66.5 %copy-start.56 = (f32[48,128]{1,0:T(8,128)S(1)}, f32[48,128]{1,0:T(8,128)}, u32[]{:S(2)}) copy-start(f32[48,128]{1,0:T(8,128)} %param.26) | copy-start | bytes 73732
  246.2 67.1 %copy-start.40 = (f32[2,768,48]{1,2,0:T(8,128)S(1)}, f32[2,768,48]{1,2,0:T(8,128)}, u32[]{:S(2)}) copy-start(f32[2,768,48]{1,2,0:T(8,128)} %param.38) | copy-start | bytes 884740
  (95 other events, 449.4 us)
